TPU v7x, 256 devices: a whole 4x4x8 slice. The times are simulated.
256 devices in a mesh: row: 16 (over x, y_lo, core), col: 16 (over y_hi, z).
Axes of the slice: x: 4, y: 4 (y_hi: 2, y_lo: 2; y = y_hi * 2 + y_lo), z: 8, core: 2. Of those that a mesh axis runs over, the one named last changes fastest.
Arguments:
- forcing_right_hand: float32 [4, 256, 2048], P(None, 'row', 'col'), may hold values from 0 to 2
- material: int32 [4, 256, 2048], P(None, 'row', 'col'), may hold values from 0 to 7
- capacity: float32 [8], replicated, may hold values from 0.3 to 3
- conductivity: float32 [8], replicated, may hold values from 0.2 to 2
- vent_open: float32 [256, 2048], P('row', 'col'), may hold values from 0.5 to 2
- partners: int32 [16, 16, 2], P('row', 'col'), may hold values from 0 to 15, as said below
- subspace_basis: bfloat16 [64, 4, 256, 2048], P(None, None, 'row', 'col'), may hold values from -0.5 to 1.5
Outputs:
- thermal_iterate: float32 [4, 256, 2048], P(None, 'row', 'col')
- defect_vector: float32 [4, 256, 2048], P(None, 'row', 'col')
- restricted_operator_blocks: float32 [16, 16, 16, 64, 64], P('row', 'col')
Inputs may be any that keep to these rules, and one draw needn't show every extreme that they name: In each round the row indices of one col index pair up: partners[q, c, k] = r whenever partners[r, c, k] = q, and q never equals r.
All inputs are finite; a program needn't handle non-finite values.
Results may differ from a plain program's by a relative error of at most 0.01.
Values may be sent and summed in bfloat16 or wider, within the bound.
A program may use at most 64 MiB of HBM per device.

v0:
```python
import jax
import jax.numpy as jnp
from jax import lax
from jax.sharding import PartitionSpec as P

ITERS = 2


highest = lax.Precision.HIGHEST
plenum_gain = 1.0


def padded_2(block, sides, width):
    for axis, dim in sides:
        count = lax.axis_size(axis)
        forward = [(i, i + 1) for i in range(count - 1)]
        backward = [(target, source) for source, target in forward]
        low = lax.ppermute(
            lax.slice_in_dim(block, block.shape[dim] - width, None, axis=dim), axis, forward
        )
        high = lax.ppermute(lax.slice_in_dim(block, 0, width, axis=dim), axis, backward)
        block = jnp.concatenate([low, block, high], axis=dim)
    return block


def harmonic(left_side, right_side):
    return 2.0 * left_side * right_side / (left_side + right_side)


def lookup(material, table):
    result = jnp.zeros(material.shape, jnp.float32)
    for class_id in range(table.shape[0]):
        result = result + jnp.where(material == class_id, table[class_id], 0.0)
    return result


def local_apply(basis_block, coef_parts):
    diagonal, upper_z, lower_z, upper_x, lower_x, upper_y, lower_y = coef_parts
    padded = jnp.pad(basis_block, ((0, 0), (1, 1), (1, 1), (1, 1)))
    beside_all = upper_z * padded[:, 2:, 1:-1, 1:-1] + lower_z * padded[:, :-2, 1:-1, 1:-1]
    beside_all = (
        beside_all + upper_x * padded[:, 1:-1, 2:, 1:-1] + lower_x * padded[:, 1:-1, :-2, 1:-1]
    )
    beside_all = (
        beside_all + upper_y * padded[:, 1:-1, 1:-1, 2:] + lower_y * padded[:, 1:-1, 1:-1, :-2]
    )
    return diagonal * basis_block - beside_all


def body(forcing_right_hand, material, capacity, conductivity, vent_open, partners, subspace_basis):
    layers = forcing_right_hand.shape[0]
    vectors = subspace_basis.shape[0]
    cells = forcing_right_hand.size
    row_count = lax.axis_size("row")
    row_at = lax.axis_index("row")
    row_numbers = jnp.arange(row_count, dtype=jnp.int32)
    conduct_field = lookup(material, conductivity)
    capacity_field = lookup(material, capacity)
    rim_conduct = padded_2(conduct_field, (("row", 1), ("col", 2)), 1)
    padded_z = jnp.pad(conduct_field, ((1, 1), (0, 0), (0, 0)))
    upper_z = harmonic(conduct_field, padded_z[2:])
    lower_z = harmonic(conduct_field, padded_z[:-2])
    upper_x = harmonic(conduct_field, rim_conduct[:, 2:, 1:-1])
    lower_x = harmonic(conduct_field, rim_conduct[:, :-2, 1:-1])
    upper_y = harmonic(conduct_field, rim_conduct[:, 1:-1, 2:])
    lower_y = harmonic(conduct_field, rim_conduct[:, 1:-1, :-2])
    own_partners = partners.reshape(-1)
    vent_rows = lax.all_gather(vent_open[None], "row", axis=0, tiled=True)
    vent_sum = jnp.zeros_like(vent_open)
    for pair_round in range(own_partners.shape[0]):
        vent_sum = vent_sum + vent_rows[own_partners[pair_round]]
    diagonal = capacity_field + upper_z + lower_z + upper_x + lower_x + upper_y + lower_y
    diagonal = diagonal.at[layers - 1].add(plenum_gain * vent_open * vent_sum)
    coef_parts = (diagonal, upper_z, lower_z, upper_x, lower_x, upper_y, lower_y)

    def operator_apply(values):
        padded = padded_2(values, (("row", 1), ("col", 2)), 1)
        stacked_z = jnp.pad(values, ((1, 1), (0, 0), (0, 0)))
        beside_all = upper_z * stacked_z[2:] + lower_z * stacked_z[:-2]
        beside_all = beside_all + upper_x * padded[:, 2:, 1:-1] + lower_x * padded[:, :-2, 1:-1]
        beside_all = beside_all + upper_y * padded[:, 1:-1, 2:] + lower_y * padded[:, 1:-1, :-2]
        result = diagonal * values - beside_all
        top_rows = lax.all_gather((vent_open * values[layers - 1])[None], "row", axis=0, tiled=True)
        coupled = jnp.zeros_like(vent_open)
        for pair_round in range(own_partners.shape[0]):
            coupled = coupled + top_rows[own_partners[pair_round]]
        return result.at[layers - 1].add(-plenum_gain * vent_open * coupled)

    basis_full = subspace_basis.astype(jnp.float32)
    basis_flat = basis_full.reshape(vectors, -1)
    own_applied = local_apply(basis_full, coef_parts)
    own_block = jnp.dot(basis_flat, own_applied.reshape(vectors, -1).T, precision=highest)
    basis_rim = padded_2(subspace_basis, (("row", 2), ("col", 3)), 1).astype(jnp.float32)
    ahead_x = -jnp.einsum(
        "azy,bzy->ab",
        basis_full[:, :, -1, :] * upper_x[:, -1, :],
        basis_rim[:, :, -1, 1:-1],
        precision=highest,
    )
    behind_x = -jnp.einsum(
        "azy,bzy->ab",
        basis_full[:, :, 0, :] * lower_x[:, 0, :],
        basis_rim[:, :, 0, 1:-1],
        precision=highest,
    )
    upper_col = -jnp.einsum(
        "azx,bzx->ab",
        basis_full[:, :, :, -1] * upper_y[:, :, -1],
        basis_rim[:, :, 1:-1, -1],
        precision=highest,
    )
    lower_col = -jnp.einsum(
        "azx,bzx->ab",
        basis_full[:, :, :, 0] * lower_y[:, :, 0],
        basis_rim[:, :, 1:-1, 0],
        precision=highest,
    )
    own_top = basis_full[:, layers - 1].reshape(vectors, -1) * vent_open.reshape(-1)
    multiplicity = jnp.zeros((row_count,), jnp.float32)
    for pair_round in range(own_partners.shape[0]):
        multiplicity = multiplicity + (row_numbers == own_partners[pair_round]).astype(jnp.float32)
    vent_flat = vent_rows.reshape(row_count, -1)
    panel = subspace_basis[:, layers - 1].reshape(1, vectors, -1)
    partner_top = (
        lax.all_gather(panel, "row", axis=0, tiled=True).astype(jnp.float32) * vent_flat[:, None, :]
    )
    blocks = -plenum_gain * jnp.einsum("as,nbs->nab", own_top, partner_top, precision=highest)
    plenum_blocks = blocks * multiplicity[:, None, None]
    own_hot = (row_numbers == row_at).astype(jnp.float32)[:, None, None]
    next_hot = (row_numbers == row_at + 1).astype(jnp.float32)[:, None, None]
    prev_hot = (row_numbers == row_at - 1).astype(jnp.float32)[:, None, None]
    galerkin_rows = own_block * own_hot + ahead_x * next_hot + behind_x * prev_hot + plenum_blocks
    factor = jnp.linalg.cholesky(own_block)

    def coarse_apply(values):
        all_rows = lax.all_gather(values[None], "row", axis=0, tiled=True)
        beside = padded_2(values[None], (("col", 0),), 1)
        along = jnp.einsum("qab,qb->a", galerkin_rows, all_rows, precision=highest)
        along = along + jnp.dot(lower_col, beside[0], precision=highest)
        return along + jnp.dot(upper_col, beside[2], precision=highest)

    def invert_galerkin_operator(right_side):
        values = jax.scipy.linalg.cho_solve((factor, True), right_side)
        values = values + jax.scipy.linalg.cho_solve(
            (factor, True), right_side - coarse_apply(values)
        )
        return values

    def remove_subspace_part(values):
        return jnp.dot(basis_flat, values.reshape(-1), precision=highest)

    def spread_subspace_values(coarse_vector):
        return jnp.dot(coarse_vector, basis_flat, precision=highest).reshape(
            forcing_right_hand.shape
        )

    thermal_iterate = spread_subspace_values(
        invert_galerkin_operator(remove_subspace_part(forcing_right_hand))
    )
    defect_vector = forcing_right_hand - operator_apply(thermal_iterate)
    conjugate_update = defect_vector - spread_subspace_values(
        invert_galerkin_operator(remove_subspace_part(operator_apply(defect_vector)))
    )
    norm_now = lax.psum(jnp.sum(defect_vector * defect_vector), ("row", "col"))
    for iteration in range(ITERS):
        applied = operator_apply(conjugate_update)
        curvature = lax.psum(jnp.sum(conjugate_update * applied), ("row", "col"))
        update_factor = norm_now / curvature
        thermal_iterate = thermal_iterate + update_factor * conjugate_update
        defect_vector = defect_vector - update_factor * applied
        if iteration + 1 < ITERS:
            norm_next = lax.psum(jnp.sum(defect_vector * defect_vector), ("row", "col"))
        if iteration + 1 < ITERS:
            correction = spread_subspace_values(
                invert_galerkin_operator(remove_subspace_part(operator_apply(defect_vector)))
            )
            conjugate_update = norm_next / norm_now * conjugate_update + defect_vector - correction
            norm_now = norm_next
    restricted_operator_blocks = (galerkin_rows / cells)[None, None]
    return (thermal_iterate, defect_vector, restricted_operator_blocks)


def solution(mesh):
    return jax.shard_map(
        body,
        mesh=mesh,
        in_specs=(
            P(None, "row", "col"),
            P(None, "row", "col"),
            P(),
            P(),
            P("row", "col"),
            P("row", "col", None),
            P(None, None, "row", "col"),
        ),
        out_specs=(P(None, "row", "col"), P(None, "row", "col"), P("row", "col", None, None, None)),
        check_vma=False,
    )
```

profile of v0, /device:TPU:1, one launch (start us, length us, event | category | flops | bytes accessed | tf_op | source)
XLA Modules:
  0.0 693.0 jit_solution(267895066664501171)
XLA Ops:
  10.8 6.2 select_add_fusion
  17.0 5.1 collective-permute-start
  43.1 18.2 %all-gather = f32[256,128]{1,0:T(8,128)S(1)} all-gather(f32[16,128]{1,0:T(8,128)S(1)} %copy-done.1), channel_id=2, replica_groups=mesh['row'=16,'col'=16] {'row'}, dimensions={0}, use_global_device_ids=true | all-gather | bytes 139264 | tf_op jit(solution)/shard_map/all_gather | solution.py:68
  83.7 5.9 add_add_fusion
  93.4 12.2 %fusion.9 = f32[64,4,16,128]{0,2,3,1:T(8,128)S(1)} fusion(f32[64,4,16,128]{0,2,3,1:T(8,128)} %convert_element_type.51, f32[4,16,128]{1,2,0:T(8,128)} %copy.103, f32[4,16,128]{1,2,0:T(8,128)S(1)} %copy.102, f32[4,16,128]{1,2,0:T(8,128)S(1)} %copy.101, f32[4,16,128]{1,2,0:T(8,128)S(1)} %copy.100, f32[4,16,128]{1,2,0:T(8,128)} %copy.99, ...), kind=kLoop, calls=%fused_computation.15 | loop fusion | flops 6815744 | bytes 4423680 | tf_op jit(solution)/shard_map/sub | solution.py:47
  110.1 5.8 cholesky.18
  117.3 4.9 custom-call.13
  129.1 28.2 %all-reduce.7 = f32[1024]{0:T(1024)S(1)} all-reduce(f32[1024]{0:T(1024)S(1)} %bitcast_dynamic-update-slice_fusion.2), channel_id=3, replica_groups=mesh['row'=16,'col'=16] {'row'}, use_global_device_ids=true, to_apply=%add.7 | all-reduce | flops 1024 | bytes 8192
  173.7 8.7 %fusion.24 = f32[16,64,64]{1,2,0:T(8,128)S(1)} fusion(bf16[16,64,2048]{2,1,0:T(8,128)(2,1)} %all-gather.11.cloned.1.call-done, f32[16,2048]{1,0:T(8,128)} %mul.418, f32[8,8,16,128]{3,2,1,0:T(8,128)} %bitcast.415, f32[16]{0:T(128)} %fusion.174, f32[2048]{0:T(1024)S(1)} %bitcast.406, f32[16]{0:T(128)} %get-tuple-element.161, f32[64,64]{0,1:T(8,128)S(1)} %copy.113, ...), kind=kOutput, calls=%fused_computation.26 | convolution fusion | flops 1615396864 | bytes 5169408 | tf_op jit(solution)/shard_map/as,nbs->nab/dot_general | solution.py:127
  194.6 5.8 collective-permute-start.13
  200.5 18.6 %all-gather.2 = f32[256,128]{1,0:T(8,128)S(1)} all-gather(f32[16,128]{1,0:T(8,128)S(1)} %fusion.170), channel_id=4, replica_groups=mesh['row'=16,'col'=16] {'row'}, dimensions={0}, use_global_device_ids=true | all-gather | bytes 139264 | tf_op jit(solution)/shard_map/all_gather | solution.py:83
  227.6 5.5 collective-permute-start.17
  233.1 19.1 %all-gather.3 = f32[256,128]{1,0:T(8,128)S(1)} all-gather(f32[16,128]{1,0:T(8,128)S(1)} %fusion.168), channel_id=5, replica_groups=mesh['row'=16,'col'=16] {'row'}, dimensions={0}, use_global_device_ids=true | all-gather | bytes 139264 | tf_op jit(solution)/shard_map/all_gather | solution.py:83
  253.8 4.9 collective-permute-start.18
  260.1 26.9 %all-reduce.8 = f32[1024]{0:T(1024)S(1)} all-reduce(f32[1024]{0:T(1024)S(1)} %bitcast_dynamic-update-slice_fusion.1), channel_id=6, replica_groups=mesh['row'=16,'col'=16] {'row'}, use_global_device_ids=true, to_apply=%add.8 | all-reduce | flops 1024 | bytes 8192
  297.7 6.1 collective-permute-start.23
  303.8 19.1 %all-gather.5 = f32[256,128]{1,0:T(8,128)S(1)} all-gather(f32[16,128]{1,0:T(8,128)S(1)} %fusion.166), channel_id=7, replica_groups=mesh['row'=16,'col'=16] {'row'}, dimensions={0}, use_global_device_ids=true | all-gather | bytes 139264 | tf_op jit(solution)/shard_map/all_gather | solution.py:83
  323.6 96.9 %all-reduce.10 = (f32[]{:T(128)}, f32[]{:T(128)}) all-reduce(f32[]{:T(128)} %get-tuple-element.95, f32[]{:T(128)} %multiply_reduce_fusion.2), channel_id=1, replica_groups=mesh['row'=16,'col'=16] {'row','col'}, use_global_device_ids=true, to_apply=%region_3.5 | all-reduce | flops 2 | bytes 16 | tf_op jit(solution)/shard_map/psum | solution.py:164
  436.2 21.2 %all-gather.6 = f32[256,128]{1,0:T(8,128)} all-gather(f32[16,128]{1,0:T(8,128)S(1)} %fusion.164), channel_id=8, replica_groups=mesh['row'=16,'col'=16] {'row'}, dimensions={0}, use_global_device_ids=true | all-gather | bytes 139264 | tf_op jit(solution)/shard_map/all_gather | solution.py:83
  457.4 74.7 %psum.30 = f32[]{:T(128)} all-reduce(f32[]{:T(128)} %get-tuple-element.93), channel_id=1, replica_groups=mesh['row'=16,'col'=16] {'row','col'}, use_global_device_ids=true, to_apply=%region_7.9 | all-reduce | flops 1 | bytes 8 | tf_op jit(solution)/shard_map/psum | solution.py:172
  539.9 27.4 %all-reduce.9 = f32[1024]{0:T(1024)S(1)} all-reduce(f32[1024]{0:T(1024)S(1)} %bitcast_dynamic-update-slice_fusion), channel_id=9, replica_groups=mesh['row'=16,'col'=16] {'row'}, use_global_device_ids=true, to_apply=%add.9 | all-reduce | flops 1024 | bytes 8192
  578.7 4.9 collective-permute-start.33
  583.6 19.2 %all-gather.8 = f32[256,128]{1,0:T(8,128)S(1)} all-gather(f32[16,128]{1,0:T(8,128)S(1)} %fusion.162), channel_id=10, replica_groups=mesh['row'=16,'col'=16] {'row'}, dimensions={0}, use_global_device_ids=true | all-gather | bytes 139264 | tf_op jit(solution)/shard_map/all_gather | solution.py:83
  604.6 79.0 %psum.31 = f32[]{:T(128)} all-reduce(f32[]{:T(128)} %multiply_reduce_fusion), channel_id=1, replica_groups=mesh['row'=16,'col'=16] {'row','col'}, use_global_device_ids=true, to_apply=%region_9.11 | all-reduce | flops 1 | bytes 8 | tf_op jit(solution)/shard_map/psum | solution.py:167
  (234 shorter events, 145.5 us)
Async XLA Ops:
  7.2 166.5 %all-gather.11.cloned.1.call-start = ((), (), s32[]{:S(2)}) async-start(), calls=%async_computation | async-start | bytes 4456448 | tf_op jit(solution)/shard_map/all_gather | solution.py:125
  17.0 59.8 %collective-permute-start = (f32[4,1,128]{2,1,0:T(1,128)S(1)}, f32[4,1,128]{2,1,0:T(1,128)S(1)}, u32[]{:S(2)}, u32[]{:S(2)}) collective-permute-start(f32[4,1,128]{2,1,0:T(1,128)S(1)} %get-tuple-element.142), channel_id=1, source_target_pairs={{16,0},{32,16},{48,32},{64,48},{80,64},{96,80},{112,96},{128,112},... | collective-permute-start | bytes 6152 | tf_op jit(solution)/shard_map/ppermute | solution.py:21
  22.2 54.7 %collective-permute-start.1 = (f32[4,1,128]{2,1,0:T(1,128)S(1)}, f32[4,1,128]{2,1,0:T(1,128)S(1)}, u32[]{:S(2)}, u32[]{:S(2)}) collective-permute-start(f32[4,1,128]{2,1,0:T(1,128)S(1)} %get-tuple-element.141), channel_id=1, source_target_pairs={{0,16},{16,32},{32,48},{48,64},{64,80},{80,96},{96,112},{112,128},... | collective-permute-start | bytes 6152 | tf_op jit(solution)/shard_map/ppermute | solution.py:18
  26.1 133.7 %collective-permute-start.4 = (bf16[64,4,1,128]{3,0,1,2:T(8,128)(2,1)}, bf16[64,4,1,128]{3,0,1,2:T(8,128)(2,1)S(1)}, u32[]{:S(2)}, u32[]{:S(2)}) collective-permute-start(bf16[64,4,1,128]{3,0,1,2:T(8,128)(2,1)} %copy.137), channel_id=1, source_target_pairs={{16,0},{32,16},{48,32},{64,48},{80,64},{96,80},{112,96},{128,112},... | collective-permute-start | bytes 196616 | tf_op jit(solution)/shard_map/ppermute | solution.py:21
  29.2 129.6 %collective-permute-start.5 = (bf16[64,4,1,128]{3,0,1,2:T(8,128)(2,1)}, bf16[64,4,1,128]{3,0,1,2:T(8,128)(2,1)}, u32[]{:S(2)}, u32[]{:S(2)}) collective-permute-start(bf16[64,4,1,128]{3,0,1,2:T(8,128)(2,1)} %copy.138), channel_id=1, source_target_pairs={{0,16},{16,32},{32,48},{48,64},{64,80},{80,96},{96,112},{112,128},... | collective-permute-start | bytes 196616 | tf_op jit(solution)/shard_map/ppermute | solution.py:18
  77.0 6.7 collective-permute-start.2
  123.0 59.8 %collective-permute-start.7 = (f32[1,64]{1,0:T(1,128)}, f32[1,64]{1,0:T(1,128)}, u32[]{:S(2)}, u32[]{:S(2)}) collective-permute-start(f32[1,64]{1,0:T(1,128)} %fusion.156), channel_id=1, source_target_pairs={{0,1},{1,2},{2,3},{3,4},{4,5},{5,6},{6,7},{7,8},{8,9},{9,10},{10,1... | collective-permute-start | bytes 776 | tf_op jit(solution)/shard_map/ppermute | solution.py:18
  127.1 56.6 %collective-permute-start.9 = (f32[1,64]{1,0:T(1,128)}, f32[1,64]{1,0:T(1,128)}, u32[]{:S(2)}, u32[]{:S(2)}) collective-permute-start(f32[1,64]{1,0:T(1,128)} %fusion.156), channel_id=1, source_target_pairs={{1,0},{2,1},{3,2},{4,3},{5,4},{6,5},{7,6},{8,7},{9,8},{10,9},{11,1... | collective-permute-start | bytes 776 | tf_op jit(solution)/shard_map/ppermute | solution.py:21
  161.4 7.7 %collective-permute-start.6 = (bf16[64,4,18,1]{0,2,1,3:T(8,128)(2,1)}, bf16[64,4,18,1]{0,2,1,3:T(8,128)(2,1)S(1)}, u32[]{:S(2)}, u32[]{:S(2)}) collective-permute-start(bf16[64,4,18,1]{0,2,1,3:T(8,128)(2,1)} %get-tuple-element.114), channel_id=1, source_target_pairs={{0,1},{1,2},{2,3},{3,4},{4,5},{5,6},{6,7},{7,8},{8,9},{9,10},{10,1... | collective-permute-start | bytes 27656 | tf_op jit(solution)/shard_map/ppermute | solution.py:18
  186.5 5.6 collective-permute-start.10
  193.3 25.8 %collective-permute-start.12 = (f32[4,18,1]{2,1,0:T(8,128)S(1)}, f32[4,18,1]{2,1,0:T(8,128)S(1)}, u32[]{:S(2)}, u32[]{:S(2)}) collective-permute-start(f32[4,18,1]{2,1,0:T(8,128)S(1)} %get-tuple-element.127), channel_id=1, source_target_pairs={{1,0},{2,1},{3,2},{4,3},{5,4},{6,5},{7,6},{8,7},{9,8},{10,9},{11,1... | collective-permute-start | bytes 872 | tf_op jit(solution)/shard_map/ppermute | solution.py:21
  194.6 24.5 %collective-permute-start.13 = (f32[4,18,1]{2,1,0:T(8,128)S(1)}, f32[4,18,1]{2,1,0:T(8,128)S(1)}, u32[]{:S(2)}, u32[]{:S(2)}) collective-permute-start(f32[4,18,1]{2,1,0:T(8,128)S(1)} %get-tuple-element.128), channel_id=1, source_target_pairs={{0,1},{1,2},{2,3},{3,4},{4,5},{5,6},{6,7},{7,8},{8,9},{9,10},{10,1... | collective-permute-start | bytes 872 | tf_op jit(solution)/shard_map/ppermute | solution.py:18
  226.3 25.8 %collective-permute-start.16 = (f32[4,18,1]{2,1,0:T(8,128)S(1)}, f32[4,18,1]{2,1,0:T(8,128)S(1)}, u32[]{:S(2)}, u32[]{:S(2)}) collective-permute-start(f32[4,18,1]{2,1,0:T(8,128)S(1)} %get-tuple-element.125), channel_id=1, source_target_pairs={{1,0},{2,1},{3,2},{4,3},{5,4},{6,5},{7,6},{8,7},{9,8},{10,9},{11,1... | collective-permute-start | bytes 872 | tf_op jit(solution)/shard_map/ppermute | solution.py:21
  227.6 24.5 %collective-permute-start.17 = (f32[4,18,1]{2,1,0:T(8,128)S(1)}, f32[4,18,1]{2,1,0:T(8,128)S(1)}, u32[]{:S(2)}, u32[]{:S(2)}) collective-permute-start(f32[4,18,1]{2,1,0:T(8,128)S(1)} %get-tuple-element.126), channel_id=1, source_target_pairs={{0,1},{1,2},{2,3},{3,4},{4,5},{5,6},{6,7},{7,8},{8,9},{9,10},{10,1... | collective-permute-start | bytes 872 | tf_op jit(solution)/shard_map/ppermute | solution.py:18
  253.8 33.7 %collective-permute-start.18 = (f32[1,64]{1,0:T(1,128)S(1)}, f32[1,64]{1,0:T(1,128)S(1)}, u32[]{:S(2)}, u32[]{:S(2)}) collective-permute-start(f32[1,64]{1,0:T(1,128)S(1)} %fusion.151), channel_id=1, source_target_pairs={{0,1},{1,2},{2,3},{3,4},{4,5},{5,6},{6,7},{7,8},{8,9},{9,10},{10,1... | collective-permute-start | bytes 776 | tf_op jit(solution)/shard_map/ppermute | solution.py:18
  258.7 29.0 %collective-permute-start.19 = (f32[1,64]{1,0:T(1,128)S(1)}, f32[1,64]{1,0:T(1,128)S(1)}, u32[]{:S(2)}, u32[]{:S(2)}) collective-permute-start(f32[1,64]{1,0:T(1,128)S(1)} %fusion.151), channel_id=1, source_target_pairs={{1,0},{2,1},{3,2},{4,3},{5,4},{6,5},{7,6},{8,7},{9,8},{10,9},{11,1... | collective-permute-start | bytes 776 | tf_op jit(solution)/shard_map/ppermute | solution.py:21
  296.4 26.5 %collective-permute-start.22 = (f32[4,18,1]{2,1,0:T(8,128)S(1)}, f32[4,18,1]{2,1,0:T(8,128)S(1)}, u32[]{:S(2)}, u32[]{:S(2)}) collective-permute-start(f32[4,18,1]{2,1,0:T(8,128)S(1)} %get-tuple-element.123), channel_id=1, source_target_pairs={{1,0},{2,1},{3,2},{4,3},{5,4},{6,5},{7,6},{8,7},{9,8},{10,9},{11,1... | collective-permute-start | bytes 872 | tf_op jit(solution)/shard_map/ppermute | solution.py:21
  297.7 25.2 %collective-permute-start.23 = (f32[4,18,1]{2,1,0:T(8,128)S(1)}, f32[4,18,1]{2,1,0:T(8,128)S(1)}, u32[]{:S(2)}, u32[]{:S(2)}) collective-permute-start(f32[4,18,1]{2,1,0:T(8,128)S(1)} %get-tuple-element.124), channel_id=1, source_target_pairs={{0,1},{1,2},{2,3},{3,4},{4,5},{5,6},{6,7},{7,8},{8,9},{9,10},{10,1... | collective-permute-start | bytes 872 | tf_op jit(solution)/shard_map/ppermute | solution.py:18
  430.3 103.2 %collective-permute-start.26 = (f32[4,18,1]{2,1,0:T(8,128)}, f32[4,18,1]{2,1,0:T(8,128)}, u32[]{:S(2)}, u32[]{:S(2)}) collective-permute-start(f32[4,18,1]{2,1,0:T(8,128)} %get-tuple-element.121), channel_id=1, source_target_pairs={{1,0},{2,1},{3,2},{4,3},{5,4},{6,5},{7,6},{8,7},{9,8},{10,9},{11,1... | collective-permute-start | bytes 872 | tf_op jit(solution)/shard_map/ppermute | solution.py:21
  431.6 101.9 %collective-permute-start.27 = (f32[4,18,1]{2,1,0:T(8,128)}, f32[4,18,1]{2,1,0:T(8,128)}, u32[]{:S(2)}, u32[]{:S(2)}) collective-permute-start(f32[4,18,1]{2,1,0:T(8,128)} %get-tuple-element.122), channel_id=1, source_target_pairs={{0,1},{1,2},{2,3},{3,4},{4,5},{5,6},{6,7},{7,8},{8,9},{9,10},{10,1... | collective-permute-start | bytes 872 | tf_op jit(solution)/shard_map/ppermute | solution.py:18
  536.7 31.1 %collective-permute-start.28 = (f32[1,64]{1,0:T(1,128)S(1)}, f32[1,64]{1,0:T(1,128)S(1)}, u32[]{:S(2)}, u32[]{:S(2)}) collective-permute-start(f32[1,64]{1,0:T(1,128)S(1)} %fusion.146), channel_id=1, source_target_pairs={{0,1},{1,2},{2,3},{3,4},{4,5},{5,6},{6,7},{7,8},{8,9},{9,10},{10,1... | collective-permute-start | bytes 776 | tf_op jit(solution)/shard_map/ppermute | solution.py:18
  538.5 30.2 %collective-permute-start.29 = (f32[1,64]{1,0:T(1,128)S(1)}, f32[1,64]{1,0:T(1,128)S(1)}, u32[]{:S(2)}, u32[]{:S(2)}) collective-permute-start(f32[1,64]{1,0:T(1,128)S(1)} %fusion.146), channel_id=1, source_target_pairs={{1,0},{2,1},{3,2},{4,3},{5,4},{6,5},{7,6},{8,7},{9,8},{10,9},{11,1... | collective-permute-start | bytes 776 | tf_op jit(solution)/shard_map/ppermute | solution.py:21
  577.4 25.4 %collective-permute-start.32 = (f32[4,18,1]{2,1,0:T(8,128)S(1)}, f32[4,18,1]{2,1,0:T(8,128)S(1)}, u32[]{:S(2)}, u32[]{:S(2)}) collective-permute-start(f32[4,18,1]{2,1,0:T(8,128)S(1)} %get-tuple-element.119), channel_id=1, source_target_pairs={{1,0},{2,1},{3,2},{4,3},{5,4},{6,5},{7,6},{8,7},{9,8},{10,9},{11,1... | collective-permute-start | bytes 872 | tf_op jit(solution)/shard_map/ppermute | solution.py:21
  578.7 24.1 %collective-permute-start.33 = (f32[4,18,1]{2,1,0:T(8,128)S(1)}, f32[4,18,1]{2,1,0:T(8,128)S(1)}, u32[]{:S(2)}, u32[]{:S(2)}) collective-permute-start(f32[4,18,1]{2,1,0:T(8,128)S(1)} %get-tuple-element.120), channel_id=1, source_target_pairs={{0,1},{1,2},{2,3},{3,4},{4,5},{5,6},{6,7},{7,8},{8,9},{9,10},{10,1... | collective-permute-start | bytes 872 | tf_op jit(solution)/shard_map/ppermute | solution.py:18
  (32 other events, 722.3 us)
Sparse Core Ops, SparseCore 0:
  9.9 44.9 all-gather.10
where the time goes:
time: 696 us; the launch traced here: 693 us
  blocking collectives  449 us (65%)
  starting transfers between devices  99.7 us (14%)
  other arithmetic  50.6 us (7%)
  matrix products  33 us (5%)
  local copies, waits for them, and re-layouts  31.7 us (5%)
  between operations  22.9 us (3%)
    all_gather x5, blocking collectives, operator_apply(): lax.all_gather((vent_open * values[layers - 1])[None], 'row', axis=0, til...  97.2 us
    psum x1, blocking collectives, body(): norm_now = lax.psum(jnp.sum(defect_vector * defect_vector), ('row', 'col'))  96.9 us
    unnamed x3, blocking collectives  82.5 us
    psum x1, blocking collectives, body(): curvature = lax.psum(jnp.sum(conjugate_update * applied), ('row', 'col'))  79 us
    psum x1, blocking collectives, body(): norm_next = lax.psum(jnp.sum(defect_vector * defect_vector), ('row', 'col'))  74.7 us
    ppermute x17, starting transfers between devices, padded_2(): lax.ppermute(lax.slice_in_dim(block, block.shape[dim] - width, None, axis...  64.6 us
    ppermute x17, starting transfers between devices, padded_2(): lax.ppermute(lax.slice_in_dim(block, 0, width, axis=dim), axis, backward)  35.1 us
    all_gather x1, blocking collectives, body(): vent_rows = lax.all_gather(vent_open[None], 'row', axis=0, tiled=True)  18.2 us
  transfers between devices with their start and end apart: 35, of which 6 were waited for; matrix products, arithmetic and copies ran while one was open for 14% of the time, Pallas kernels for 0%

commit v1 on v0

v1 whole, which is shorter than its diff:
```python
import functools

import jax
import jax.numpy as jnp
from jax import lax
from jax.experimental import pallas as pl
from jax.experimental.pallas import tpu as pltpu
from jax.sharding import PartitionSpec as P

MESH = pl.DeviceIdType.MESH
F32, BF16 = jnp.float32, jnp.bfloat16
LANES = 128
PIVOTS = 4
ROUNDS = 9


def harmonic(left_side, right_side):
    return 2.0 * left_side * right_side / (left_side + right_side)


def split(values):
    high = values.astype(BF16)
    return high, (values - high.astype(F32)).astype(BF16)


def dot_t(left, right):
    return lax.dot_general(left, right, (((1,), (1,)), ((), ())), preferred_element_type=F32)


def inverse(matrix):
    n = matrix.shape[0]
    row_id = lax.broadcasted_iota(jnp.int32, (n, n), 0)
    col_id = lax.broadcasted_iota(jnp.int32, (n, n), 1)
    work = jnp.concatenate([matrix, (row_id == col_id).astype(F32)], axis=1)
    wide_row = lax.broadcasted_iota(jnp.int32, work.shape, 0)
    for base in range(0, n, PIVOTS):
        ids = range(PIVOTS)
        rows = [work[base + i : base + i + 1, :] for i in ids]
        pivot = [
            [jnp.broadcast_to(rows[i][:, base + j : base + j + 1], rows[i].shape) for j in ids]
            for i in ids
        ]
        inside = (wide_row >= base) & (wide_row < base + PIVOTS)
        columns = [
            jnp.where(
                inside,
                jnp.where(wide_row == base + j, -1.0, 0.0),
                jnp.broadcast_to(work[:, base + j : base + j + 1], work.shape),
            )
            for j in ids
        ]
        work = jnp.where(inside, 0.0, work)
        for p in ids:
            scale = 1.0 / pivot[p][p]
            rows[p] = rows[p] * scale
            for j in range(p + 1, PIVOTS):
                pivot[p][j] = pivot[p][j] * scale
            for i in ids:
                if i != p:
                    factor = pivot[i][p]
                    rows[i] = rows[i] - factor * rows[p]
                    for j in range(p + 1, PIVOTS):
                        pivot[i][j] = pivot[i][j] - factor * pivot[p][j]
        for j in ids:
            work = work - columns[j] * rows[j]
    return work[:, n:]


def kernel(
    n_row, n_col,
    cap_ref, con_ref, par_ref, rhs_ref, mat_ref, vent_ref, basis_ref,
    x_ref, r_ref, e_ref,
    fields, ysend, yrecv, info, zf, zk, zr, az, xb, pa, pb, pc, coef, work, wide, inv_ref,
    red_row, red_col,
    top_s, top_r, x_s, x_r, y_s, y_r, info_s, info_r, xb_s, xb_r, pa_s, pa_r, pc_s, pc_r,
    rr_s, rr_r, rc_s, rc_r, *tops,
):
    layers, width, depth = rhs_ref.shape
    vectors = basis_ref.shape[0]
    lines = layers * width
    share = width // n_row
    row, col = lax.axis_index("row"), lax.axis_index("col")
    row_up, row_dn = lax.rem(row + 1, n_row), lax.rem(row + n_row - 1, n_row)
    col_up, col_dn = lax.rem(col + 1, n_col), lax.rem(col + n_col - 1, n_col)

    def peer(i, me, count):
        return lax.rem(me + i, count)

    def remote(src, dst, send, recv, target):
        return pltpu.make_async_remote_copy(
            src_ref=src, dst_ref=dst, send_sem=send, recv_sem=recv,
            device_id=target, device_id_type=MESH,
        )

    def wait_bytes(ref, sem):
        pltpu.make_async_copy(ref, ref, sem).wait()

    barrier = pltpu.get_barrier_semaphore()

    @pl.loop(1, n_row)
    def _(i):
        pl.semaphore_signal(
            barrier, inc=1, device_id=(peer(i, row, n_row), col), device_id_type=MESH
        )

    @pl.loop(1, n_col)
    def _(i):
        pl.semaphore_signal(
            barrier, inc=1, device_id=(row, peer(i, col, n_col)), device_id_type=MESH
        )

    material = mat_ref[...]
    conduct = jnp.zeros(material.shape, F32)
    heat = jnp.zeros(material.shape, F32)
    for class_id in range(con_ref.shape[0]):
        hit = material == class_id
        conduct = jnp.where(hit, con_ref[class_id], conduct)
        heat = jnp.where(hit, cap_ref[class_id], heat)
    vent = vent_ref[...]
    partner = [par_ref[k] for k in range(2)]
    info_row = lax.broadcasted_iota(jnp.int32, (8, LANES), 0)
    info[row] = jnp.where(
        info_row == 0, partner[0].astype(F32), jnp.where(info_row == 1, partner[1].astype(F32), 0.0)
    )
    lane = lax.broadcasted_iota(jnp.int32, (8, LANES), 1)
    groups = lines // 8

    def start_exchange(at, values, top):
        fields[at, :, 8 : 8 + width, :] = values
        tops[at][row] = top
        tiles = values.reshape(groups, 8, depth)
        packed = jnp.zeros((8, LANES), F32)
        for j in range(groups):
            packed = jnp.where(lane == j, pltpu.roll(tiles[j], j, 1), packed)
            packed = jnp.where(
                lane == groups + j, pltpu.roll(tiles[j], groups + j + 1, 1), packed
            )
        ysend[at] = packed

        @pl.loop(1, n_row)
        def _(i):
            remote(
                tops[at].at[row], tops[at].at[row], top_s.at[at], top_r.at[at],
                (peer(i, row, n_row), col),
            ).start()

        for copy in side_copies(at):
            copy.start()

    def side_copies(at):
        return (
            remote(
                fields.at[at, :, pl.ds(7 + width, 1), :], fields.at[at, :, pl.ds(7, 1), :],
                x_s.at[at, 0], x_r.at[at, 0], (row_up, col),
            ),
            remote(
                fields.at[at, :, pl.ds(8, 1), :], fields.at[at, :, pl.ds(8 + width, 1), :],
                x_s.at[at, 1], x_r.at[at, 1], (row_dn, col),
            ),
            remote(ysend.at[at], yrecv.at[at, 0], y_s.at[at, 0], y_r.at[at, 0], (row, col_up)),
            remote(ysend.at[at], yrecv.at[at, 1], y_s.at[at, 1], y_r.at[at, 1], (row, col_dn)),
        )

    def finish_exchange(at, values):
        for copy in side_copies(at):
            copy.wait_recv()
        wait_bytes(tops[at].at[pl.ds(0, n_row - 1)], top_r.at[at])
        tiles = values.reshape(groups, 8, depth)
        from_dn, from_up = yrecv[at, 0], yrecv[at, 1]
        dn_y, up_y = [], []
        for j in range(groups):
            dn_y.append(
                pltpu.roll(
                    jnp.where(
                        lane == LANES - 1, pltpu.roll(from_dn, LANES - 1 - groups - j, 1), tiles[j]
                    ),
                    1, 1,
                )
            )
            up_y.append(
                pltpu.roll(
                    jnp.where(lane == 0, pltpu.roll(from_up, (LANES - j) % LANES, 1), tiles[j]),
                    LANES - 1, 1,
                )
            )
        dn_y = jnp.stack(dn_y).reshape(values.shape)
        up_y = jnp.stack(up_y).reshape(values.shape)
        dn_x = fields[at, :, 7 : 7 + width, :]
        up_x = fields[at, :, 9 : 9 + width, :]
        coupled = tops[at][partner[0]] + tops[at][partner[1]]
        return up_x, dn_x, up_y, dn_y, coupled

    pl.semaphore_wait(barrier, n_row - 1 + n_col - 1)
    start_exchange(0, conduct, vent)

    @pl.loop(1, n_row)
    def _(i):
        remote(info.at[row], info.at[row], info_s, info_r, (peer(i, row, n_row), col)).start()

    @pl.loop(0, vectors)
    def _(a):
        zf[pl.ds(a * lines, lines), :] = basis_ref[a].astype(F32)

    pad = width * vectors
    zk[0:pad, :] = jnp.zeros((pad, depth), F32)
    zk[pad + lines * vectors :, :] = jnp.zeros((pad, depth), F32)

    def line(k):
        return pl.ds(pad + k * vectors, vectors)

    @pl.loop(0, lines)
    def _(k):
        block = zf[pl.ds(k, vectors, stride=lines), :]
        zk[line(k), :] = block
        zr[:, pl.ds(pl.multiple_of(k * depth, depth), depth)] = block.astype(BF16)

    def cells(k):
        return pl.ds(pl.multiple_of(k * depth, depth), depth)

    def face_copies():
        copies = []
        for z in range(layers):
            there = pl.ds(z * depth, depth)
            copies.append(
                remote(
                    zr.at[:, cells(z * width + width - 1)], xb.at[0, :, there],
                    xb_s.at[0, z], xb_r.at[0, z], (row_up, col),
                )
            )
            copies.append(
                remote(
                    zr.at[:, cells(z * width)], xb.at[1, :, there],
                    xb_s.at[1, z], xb_r.at[1, z], (row_dn, col),
                )
            )
        return copies

    top_line = (layers - 1) * width
    for copy in face_copies():
        copy.start()

    @pl.loop(1, n_row)
    def _(i):
        target = peer(i, row, n_row)
        first = top_line + target * share
        remote(
            zr.at[:, pl.ds(pl.multiple_of(first * depth, depth), share * depth)], pa.at[row],
            pa_s, pa_r, (target, col),
        ).start()

    def project(values):
        work[...] = values.reshape(lines, depth)

        def step(k, total):
            return total + zk[line(k), :] * work[pl.ds(k, 1), :]

        total = lax.fori_loop(0, lines, step, jnp.zeros((vectors, depth), F32), unroll=8)
        return jnp.sum(total, axis=1, keepdims=True)

    def expand(coarse):
        wide[...] = jnp.broadcast_to(coarse, wide.shape)

        def step(a, total):
            return total + zf[pl.ds(a * lines, lines), :] * wide[pl.ds(a, 1), :]

        total = lax.fori_loop(0, vectors, step, jnp.zeros((lines, depth), F32), unroll=8)
        return total.reshape(layers, width, depth)

    square_row = lax.broadcasted_iota(jnp.int32, (vectors, vectors), 0)
    square_col = lax.broadcasted_iota(jnp.int32, (vectors, vectors), 1)

    def solve(right_side):
        flat = jnp.sum(jnp.where(square_row == square_col, right_side, 0.0), axis=0, keepdims=True)
        return jnp.sum(inv_ref[...] * flat, axis=1, keepdims=True)

    rhs = rhs_ref[...]
    first_side = project(rhs)

    near = finish_exchange(0, conduct)
    none = jnp.zeros((1, width, depth), F32)
    up_z = jnp.concatenate([harmonic(conduct[:-1], conduct[1:]), none], axis=0)
    dn_z = jnp.concatenate([none, up_z[:-1]], axis=0)
    x_id = lax.broadcasted_iota(jnp.int32, conduct.shape, 1)
    y_id = lax.broadcasted_iota(jnp.int32, conduct.shape, 2)
    x_last, x_first = x_id == width - 1, x_id == 0
    y_last, y_first = y_id == depth - 1, y_id == 0
    up_x = jnp.where(x_last & (row == n_row - 1), 0.0, harmonic(conduct, near[0]))
    dn_x = jnp.where(x_first & (row == 0), 0.0, harmonic(conduct, near[1]))
    up_y = jnp.where(y_last & (col == n_col - 1), 0.0, harmonic(conduct, near[2]))
    dn_y = jnp.where(y_first & (col == 0), 0.0, harmonic(conduct, near[3]))
    diagonal = heat + up_z + dn_z + up_x + dn_x + up_y + dn_y
    diagonal = jnp.concatenate(
        [diagonal[:-1], (diagonal[-1] + vent * near[4])[None]], axis=0
    )

    local = (
        diagonal, up_z, dn_z,
        jnp.where(x_last, 0.0, up_x), jnp.where(x_first, 0.0, dn_x),
        jnp.where(y_last, 0.0, up_y), jnp.where(y_first, 0.0, dn_y),
    )
    for c in range(7):
        coef[c] = local[c].reshape(lines, depth)

    @pl.loop(0, lines)
    def _(k):
        own = zk[line(k), :]

        def at(c):
            return coef[c, pl.ds(k, 1), :]

        applied = at(0) * own
        applied = applied - at(1) * zk[line(k + width), :] - at(2) * zk[line(k - width), :]
        applied = applied - at(3) * zk[line(k + 1), :] - at(4) * zk[line(k - 1), :]
        applied = applied - at(5) * pltpu.roll(own, depth - 1, 1) - at(6) * pltpu.roll(own, 1, 1)
        high, low = split(applied)
        az[0:vectors, cells(k)] = high
        az[vectors : 2 * vectors, cells(k)] = low

    both = dot_t(az[...], zr[...])
    own_block = both[:vectors] + both[vectors:]
    inv_ref[...] = inverse(own_block)

    def apply_start(at, values):
        start_exchange(at, values, vent * values[layers - 1])

    def apply_finish(at, values):
        near = finish_exchange(at, values)
        none = jnp.zeros((1, width, depth), F32)
        result = diagonal * values
        result = result - up_z * jnp.concatenate([values[1:], none], axis=0)
        result = result - dn_z * jnp.concatenate([none, values[:-1]], axis=0)
        result = result - up_x * near[0] - dn_x * near[1] - up_y * near[2] - dn_y * near[3]
        return jnp.concatenate([result[:-1], (result[-1] - vent * near[4])[None]], axis=0)

    def apply(at, values, beside=None):
        apply_start(at, values)
        if beside is not None:
            beside()
        return apply_finish(at, values)

    def correct(at, right_side, besides):
        first = expand(solve(right_side))
        first_image = apply(at, first, besides[0])
        second = expand(solve(right_side - project(first_image)))
        second_image = apply(at + 1, second, besides[1])
        return first + second, first_image + second_image

    def faces():
        for copy in face_copies():
            copy.wait_recv()
        for side, at, coefficient in ((0, 0, dn_x), (1, width - 1, up_x)):
            terms = [
                zk[line(z * width + at), :] * coefficient[z, at : at + 1, :] for z in range(layers)
            ]
            high, low = split(jnp.concatenate(terms, axis=1))
            both = dot_t(jnp.concatenate([high, low], axis=0), xb[side])
            wide_faces[side] = both[:vectors] + both[vectors:]

    wide_faces = [None, None]

    def plenum():
        wait_bytes(info.at[pl.ds(0, n_row - 1)], info_r)
        wait_bytes(pa.at[pl.ds(0, n_row - 1)], pa_r)
        first = top_line + row * share
        pa[row] = zr[:, pl.ds(pl.multiple_of(first * depth, depth), share * depth)]

        @pl.loop(0, n_row)
        def _(s):
            own = pa[s]
            total = None
            for i in range(share):
                rows = []
                for k in range(2):
                    which = info[s, k : k + 1, :]
                    chosen = jnp.zeros((vectors, depth), F32)
                    gain = jnp.zeros((1, depth), F32)
                    for t in range(n_row):
                        block = pa[t, :, i * depth : (i + 1) * depth].astype(F32)
                        gain = jnp.where(which == t, tops[0][t, pl.ds(row * share + i, 1), :], gain)
                        chosen = jnp.where(which == t, block, chosen)
                    rows.append(chosen * (gain * tops[0][s, pl.ds(row * share + i, 1), :]))
                high, low = split(jnp.concatenate(rows, axis=0))
                mine = own[:, i * depth : (i + 1) * depth]
                part = dot_t(
                    jnp.concatenate([mine, mine], axis=1), jnp.concatenate([high, low], axis=1)
                )
                total = part if total is None else total + part
            pb[s] = total

        @pl.loop(1, n_row)
        def _(i):
            target = peer(i, row, n_row)
            remote(pb.at[target], pc.at[row], pc_s, pc_r, (target, col)).start()

        pc[row] = pb[row]

    def finish_blocks():
        wait_bytes(pc.at[pl.ds(0, n_row - 1)], pc_r)
        total = lax.fori_loop(
            0, n_row, lambda i, t: t + pc[i], jnp.zeros((vectors, 2 * vectors), F32)
        )
        scale = 1.0 / (lines * depth)
        parts = (
            own_block * scale, wide_faces[0] * -scale, wide_faces[1] * -scale,
            total[:, :vectors] * -scale, total[:, vectors:] * -scale,
        )

        @pl.loop(0, n_row)
        def _(q):
            hits = (q == row, q == row - 1, q == row + 1, q == partner[0], q == partner[1])
            value = jnp.zeros((vectors, vectors), F32)
            for hit, part in zip(hits, parts):
                value = value + jnp.where(hit, 1.0, 0.0) * part
            e_ref[q] = value

    iterate, image = correct(1, first_side, (faces, None))
    defect = rhs - image
    turned = apply(3, defect)
    shift, image = correct(4, project(turned), (plenum, None))
    direction, stepped = defect - shift, turned - image
    turned = apply(6, stepped)
    shift, image = correct(7, project(turned), (None, finish_blocks))
    slanted, slanted_image = stepped - shift, turned - image

    def lanes_of(left, right):
        return jnp.sum((left * right).reshape(lines, depth), axis=0, keepdims=True)

    sums = [
        lanes_of(defect, defect), lanes_of(direction, stepped), lanes_of(defect, stepped),
        lanes_of(stepped, stepped), lanes_of(slanted, stepped), lanes_of(slanted, slanted_image),
    ]
    red_row[row] = jnp.concatenate(sums + [jnp.zeros((2, depth), F32)], axis=0)

    @pl.loop(1, n_row)
    def _(i):
        remote(red_row.at[row], red_row.at[row], rr_s, rr_r, (peer(i, row, n_row), col)).start()

    wait_bytes(red_row.at[pl.ds(0, n_row - 1)], rr_r)
    red_col[col] = jnp.sum(red_row[...], axis=0)

    @pl.loop(1, n_col)
    def _(i):
        remote(red_col.at[col], red_col.at[col], rc_s, rc_r, (row, peer(i, col, n_col))).start()

    wait_bytes(red_col.at[pl.ds(0, n_col - 1)], rc_r)
    scalars = jnp.sum(jnp.sum(red_col[...], axis=0), axis=1, keepdims=True)
    norm, curve, cross, square, mixed, slant = [scalars[i : i + 1, :] for i in range(6)]
    alpha = norm / curve
    after = norm - 2.0 * alpha * cross + alpha * alpha * square
    more = 1.0 + after / norm
    curve = more * more * curve - 2.0 * more * alpha * mixed + alpha * alpha * slant
    last = after / curve

    def scaled(factor, values):
        return jnp.broadcast_to(factor, values.shape) * values

    alpha, more, last = alpha[None], more[None], last[None]
    x_ref[...] = (
        iterate
        + scaled(alpha, direction)
        + scaled(last, scaled(more, direction) - scaled(alpha, slanted))
    )
    r_ref[...] = (
        defect
        - scaled(alpha, stepped)
        - scaled(last, scaled(more, stepped) - scaled(alpha, slanted_image))
    )

    for at in range(ROUNDS):
        for copy in side_copies(at):
            copy.wait_send()
        wait_bytes(tops[at].at[pl.ds(0, n_row - 1)], top_s.at[at])

    for copy in face_copies():
        copy.wait_send()
    wait_bytes(info.at[pl.ds(0, n_row - 1)], info_s)
    wait_bytes(pa.at[pl.ds(0, n_row - 1)], pa_s)
    wait_bytes(pc.at[pl.ds(0, n_row - 1)], pc_s)
    wait_bytes(red_row.at[pl.ds(0, n_row - 1)], rr_s)
    wait_bytes(red_col.at[pl.ds(0, n_col - 1)], rc_s)


def body(n_row, n_col, rhs, material, capacity, conductivity, vent, partners, basis):
    layers, width, depth = rhs.shape
    vectors = basis.shape[0]
    lines, share = layers * width, width // n_row
    smem, vmem = pl.BlockSpec(memory_space=pltpu.SMEM), pl.BlockSpec(memory_space=pltpu.VMEM)
    dma = pltpu.SemaphoreType.DMA
    scratch = [
        pltpu.VMEM((ROUNDS, layers, width + 16, depth), F32),
        pltpu.VMEM((ROUNDS, 8, LANES), F32),
        pltpu.VMEM((ROUNDS, 2, 8, LANES), F32),
        pltpu.VMEM((n_row, 8, LANES), F32),
        pltpu.VMEM((vectors * lines, depth), F32),
        pltpu.VMEM((vectors * (lines + 2 * width), depth), F32),
        pltpu.VMEM((vectors, lines * depth), BF16),
        pltpu.VMEM((2 * vectors, lines * depth), BF16),
        pltpu.VMEM((2, vectors, layers * depth), BF16),
        pltpu.VMEM((n_row, vectors, share * depth), BF16),
        pltpu.VMEM((n_row, vectors, 2 * vectors), F32),
        pltpu.VMEM((n_row, vectors, 2 * vectors), F32),
        pltpu.VMEM((7, lines, depth), F32),
        pltpu.VMEM((lines, depth), F32),
        pltpu.VMEM((vectors, depth), F32),
        pltpu.VMEM((vectors, vectors), F32),
        pltpu.VMEM((n_row, 8, LANES), F32),
        pltpu.VMEM((n_col, 8, LANES), F32),
        dma((ROUNDS,)), dma((ROUNDS,)), dma((ROUNDS, 2)), dma((ROUNDS, 2)),
        dma((ROUNDS, 2)), dma((ROUNDS, 2)), dma, dma, dma((2, layers)), dma((2, layers)),
        dma, dma, dma, dma, dma, dma, dma, dma,
        *[pltpu.VMEM((n_row, width, depth), F32) for _ in range(ROUNDS)],
    ]
    iterate, defect, blocks = pl.pallas_call(
        functools.partial(kernel, n_row, n_col),
        out_shape=(
            jax.ShapeDtypeStruct(rhs.shape, F32),
            jax.ShapeDtypeStruct(rhs.shape, F32),
            jax.ShapeDtypeStruct((n_row, vectors, vectors), F32),
        ),
        in_specs=[smem, smem, smem, vmem, vmem, vmem, vmem],
        out_specs=(vmem, vmem, vmem),
        scratch_shapes=scratch,
        compiler_params=pltpu.CompilerParams(
            collective_id=0, has_side_effects=True, vmem_limit_bytes=48 * 1024 * 1024
        ),
        name="deflated_cg",
    )(
        capacity, conductivity, partners.reshape(-1), rhs, material, vent,
        basis.reshape(vectors, lines, depth),
    )
    return iterate, defect, blocks[None, None]


def solution(mesh):
    n_row, n_col = mesh.shape["row"], mesh.shape["col"]
    return jax.shard_map(
        functools.partial(body, n_row, n_col),
        mesh=mesh,
        in_specs=(
            P(None, "row", "col"),
            P(None, "row", "col"),
            P(),
            P(),
            P("row", "col"),
            P("row", "col", None),
            P(None, None, "row", "col"),
        ),
        out_specs=(P(None, "row", "col"), P(None, "row", "col"), P("row", "col", None, None, None)),
        check_vma=False,
    )
```

time: 696 us -> 88.9 us (0.13)
  blocking collectives: 449 us -> 0 us
  starting transfers between devices: 99.7 us -> 0 us
  Pallas kernels: 0 us -> 81.8 us
  other arithmetic: 50.6 us -> 0 us
  matrix products: 33 us -> 0 us
  local copies, waits for them, and re-layouts: 31.7 us -> 6.12 us
  between operations: 22.9 us -> 0.67 us
    psum x3 -> x0, blocking collectives: 251 us -> none  [the longest x1 96.9 us: body(): norm_now = lax.psum(jnp.sum(defect_vector * defect_vector), ('row', 'col'))]
    all_gather x6 -> x0, blocking collectives: 115 us -> none  [the longest x5 97.2 us: operator_apply(): lax.all_gather((vent_open * values[layers - 1])[None], 'row', axis=0, til...]
    ppermute x34 -> x0, starting transfers between devices: 99.7 us -> none  [the longest x17 64.6 us: padded_2(): lax.ppermute(lax.slice_in_dim(block, block.shape[dim] - width, None, axis...]
    unnamed x3 -> x0, blocking collectives: 82.5 us -> none
    pallas_call x0 -> x1, Pallas kernels: none -> 81.8 us  [body(): pl.pallas_call(functools.partial(kernel, n_row, n_col), out_shape=(jax.Sh...]
    dot_general x21 -> x0, matrix products: 30 us -> none  [the longest x1 8.68 us: body(): jnp.einsum('as,nbs->nab', own_top, partner_top, precision=highest)]
    sub x9 -> x0, other arithmetic: 14.2 us -> none  [the longest x1 12.2 us: local_apply(): return diagonal * basis_block - beside_all]
    add x3 -> x0, other arithmetic: 12.7 us -> none  [the longest x1 6.2 us: lookup(): result = result + jnp.where(material == class_id, table[class_id], 0.0)]
  transfers between devices with their start and end apart: 35 -> 0, of which waited for: 6 -> 0; matrix products, arithmetic and copies ran while one was open for 14% -> 0% of each run, Pallas kernels for 0% -> 0%
where the time goes in v1:
time: 88.9 us; the launch traced here: 88.6 us
  Pallas kernels  81.8 us (92%)
  local copies, waits for them, and re-layouts  6.12 us (7%)
    pallas_call x1, Pallas kernels, body(): pl.pallas_call(functools.partial(kernel, n_row, n_col), out_shape=(jax.Sh...  81.8 us
    unnamed x17, local copies, waits for them, and re-layouts  6.12 us

profile of v1, /device:TPU:1, one launch (start us, length us, event | category | flops | bytes accessed | tf_op | source)
XLA Modules:
  0.0 88.6 jit_solution(16956989721105010956)
XLA Ops:
  0.6 0.0 copy-start.4
  0.6 0.0 copy-start.5
  0.7 0.0 copy-start.6
  0.7 0.6 copy-done.4
  1.3 0.0 copy-done.5
  1.3 0.0 copy-done.6
  1.3 0.0 copy-start
  1.3 1.2 %copy-done = bf16[64,4,16,128]{3,2,1,0:T(8,128)(2,1)S(1)} copy-done((bf16[64,4,16,128]{3,2,1,0:T(8,128)(2,1)S(1)}, bf16[64,4,16,128]{3,2,1,0:T(8,128)(2,1)}, u32[]{:S(2)}) %copy-start) | copy-done | bytes 1048600
  2.5 0.0 copy-start.1
  2.5 0.8 copy-done.1
  3.3 0.0 copy-start.2
  3.3 0.8 copy-done.2
  4.1 0.0 copy-start.3
  4.1 0.7 copy-done.3
  4.8 81.8 %deflated_cg.1 = (f32[4,16,128]{2,1,0:T(8,128)S(1)}, f32[4,16,128]{2,1,0:T(8,128)S(1)}, f32[16,64,64]{2,1,0:T(8,128)S(1)}) custom-call(f32[8]{0:T(128)S(1)} %copy-done.4, f32[8]{0:T(128)S(1)} %copy-done.5, s32[2]{0:T(128)S(1)} %bitcast.5, f32[4,16,128]{2,1,0:T(8,128)S(1)} %copy-done.1, s32[4,16,128]{2,1,0:T(8,128)S(1)} %copy-done.2, ...), custom_call_target="tpu_custom_call" | custom-call | tf_op jit(solution)/shard_map/deflated_cg/pallas_call | solution.py:513
  86.5 0.6 copy.13
  87.1 0.6 copy.14
  87.8 0.8 copy.15
Async XLA Ops:
  0.6 0.7 copy-start.4
  0.6 0.7 copy-start.5
  0.7 0.7 copy-start.6
  1.3 1.2 %copy-start = (bf16[64,4,16,128]{3,2,1,0:T(8,128)(2,1)S(1)}, bf16[64,4,16,128]{3,2,1,0:T(8,128)(2,1)}, u32[]{:S(2)}) copy-start(bf16[64,4,16,128]{3,2,1,0:T(8,128)(2,1)} %param.13) | copy-start | bytes 3145732
  2.5 0.8 copy-start.1
  3.3 0.8 copy-start.2
  4.1 0.7 copy-start.3

commit v2 on v1

--- a/solution.py
+++ b/solution.py
@@ -12,6 +12,7 @@
 LANES = 128
 PIVOTS = 4
 ROUNDS = 9
+PITCH = 72
 
 
 def harmonic(left_side, right_side):
@@ -68,10 +69,11 @@
 
 def kernel(
     n_row, n_col,
-    cap_ref, con_ref, par_ref, rhs_ref, mat_ref, vent_ref, basis_ref,
+    cap_ref, con_ref, par_ref, rhs_hbm, mat_hbm, vent_hbm, basis_hbm,
     x_ref, r_ref, e_ref,
-    fields, ysend, yrecv, info, zf, zk, zr, az, xb, pa, pb, pc, coef, work, wide, inv_ref,
-    red_row, red_col,
+    rhs_ref, mat_ref, vent_ref, basis_ref,
+    fields, ysend, yrecv, info, zf, zk, zr, yb, az, xb, pa, pb, pc, coef, zo, work, wide, inv_ref,
+    red_row, red_col, load,
     top_s, top_r, x_s, x_r, y_s, y_r, info_s, info_r, xb_s, xb_r, pa_s, pa_r, pc_s, pc_r,
     rr_s, rr_r, rc_s, rc_r, *tops,
 ):
@@ -83,6 +85,8 @@
     row_up, row_dn = lax.rem(row + 1, n_row), lax.rem(row + n_row - 1, n_row)
     col_up, col_dn = lax.rem(col + 1, n_col), lax.rem(col + n_col - 1, n_col)
 
+    order = sorted(range(1, n_row), key=lambda i: min(i, n_row - i), reverse=True)
+
     def peer(i, me, count):
         return lax.rem(me + i, count)
 
@@ -103,11 +107,22 @@
             barrier, inc=1, device_id=(peer(i, row, n_row), col), device_id_type=MESH
         )
 
-    @pl.loop(1, n_col)
-    def _(i):
-        pl.semaphore_signal(
-            barrier, inc=1, device_id=(row, peer(i, col, n_col)), device_id_type=MESH
-        )
+    for neighbour in (col_up, col_dn):
+        pl.semaphore_signal(barrier, inc=1, device_id=(row, neighbour), device_id_type=MESH)
+
+    loads = [
+        pltpu.make_async_copy(src, dst, load.at[i])
+        for i, (src, dst) in enumerate(
+            (
+                (mat_hbm, mat_ref), (vent_hbm, vent_ref),
+                (rhs_hbm, rhs_ref), (basis_hbm, basis_ref),
+            )
+        )
+    ]
+    for copy in loads:
+        copy.start()
+    for copy in loads[:2]:
+        copy.wait()
 
     material = mat_ref[...]
     conduct = jnp.zeros(material.shape, F32)
@@ -122,32 +137,39 @@
     info[row] = jnp.where(
         info_row == 0, partner[0].astype(F32), jnp.where(info_row == 1, partner[1].astype(F32), 0.0)
     )
-    lane = lax.broadcasted_iota(jnp.int32, (8, LANES), 1)
-    groups = lines // 8
-
-    def start_exchange(at, values, top):
-        fields[at, :, 8 : 8 + width, :] = values
+    line_id = lax.broadcasted_iota(jnp.int32, (lines, depth), 0)
+    lane_id = lax.broadcasted_iota(jnp.int32, (lines, depth), 1)
+    on_first, on_last = lane_id == line_id, lane_id == line_id + lines
+
+    def pack_sides(first, last):
+        spread = jnp.where(on_first, first, 0.0) + jnp.where(on_last, last, 0.0)
+        return jnp.sum(spread, axis=0, keepdims=True)
+
+    def send_sides(at, packed):
+        ysend[at] = jnp.broadcast_to(packed, (8, LANES))
+        for copy in y_copies(at):
+            copy.start()
+
+    def send_top(at, top):
         tops[at][row] = top
-        tiles = values.reshape(groups, 8, depth)
-        packed = jnp.zeros((8, LANES), F32)
-        for j in range(groups):
-            packed = jnp.where(lane == j, pltpu.roll(tiles[j], j, 1), packed)
-            packed = jnp.where(
-                lane == groups + j, pltpu.roll(tiles[j], groups + j + 1, 1), packed
-            )
-        ysend[at] = packed
-
-        @pl.loop(1, n_row)
-        def _(i):
+        for i in order:
             remote(
                 tops[at].at[row], tops[at].at[row], top_s.at[at], top_r.at[at],
                 (peer(i, row, n_row), col),
             ).start()
 
-        for copy in side_copies(at):
+    def send_lines(at, values):
+        fields[at, :, 8 : 8 + width, :] = values
+        for copy in x_copies(at):
             copy.start()
 
-    def side_copies(at):
+    def start_exchange(at, values, top):
+        flat = values.reshape(lines, depth)
+        send_sides(at, pack_sides(flat[:, 0:1], flat[:, depth - 1 : depth]))
+        send_top(at, top)
+        send_lines(at, values)
+
+    def x_copies(at):
         return (
             remote(
                 fields.at[at, :, pl.ds(7 + width, 1), :], fields.at[at, :, pl.ds(7, 1), :],
@@ -157,62 +179,65 @@
                 fields.at[at, :, pl.ds(8, 1), :], fields.at[at, :, pl.ds(8 + width, 1), :],
                 x_s.at[at, 1], x_r.at[at, 1], (row_dn, col),
             ),
+        )
+
+    def y_copies(at):
+        return (
             remote(ysend.at[at], yrecv.at[at, 0], y_s.at[at, 0], y_r.at[at, 0], (row, col_up)),
             remote(ysend.at[at], yrecv.at[at, 1], y_s.at[at, 1], y_r.at[at, 1], (row, col_dn)),
         )
 
     def finish_exchange(at, values):
-        for copy in side_copies(at):
+        for copy in x_copies(at):
             copy.wait_recv()
         wait_bytes(tops[at].at[pl.ds(0, n_row - 1)], top_r.at[at])
-        tiles = values.reshape(groups, 8, depth)
-        from_dn, from_up = yrecv[at, 0], yrecv[at, 1]
-        dn_y, up_y = [], []
-        for j in range(groups):
-            dn_y.append(
-                pltpu.roll(
-                    jnp.where(
-                        lane == LANES - 1, pltpu.roll(from_dn, LANES - 1 - groups - j, 1), tiles[j]
-                    ),
-                    1, 1,
-                )
-            )
-            up_y.append(
-                pltpu.roll(
-                    jnp.where(lane == 0, pltpu.roll(from_up, (LANES - j) % LANES, 1), tiles[j]),
-                    LANES - 1, 1,
-                )
-            )
-        dn_y = jnp.stack(dn_y).reshape(values.shape)
-        up_y = jnp.stack(up_y).reshape(values.shape)
+        for copy in y_copies(at):
+            copy.wait_recv()
+        flat = values.reshape(lines, depth)
+        from_dn = jnp.where(on_last, yrecv[at, 0, 0:1, :], 0.0)
+        from_up = jnp.where(on_first, yrecv[at, 1, 0:1, :], 0.0)
+        dn_y = jnp.where(
+            lane_id == 0, jnp.sum(from_dn, axis=1, keepdims=True), pltpu.roll(flat, 1, 1)
+        ).reshape(values.shape)
+        up_y = jnp.where(
+            lane_id == depth - 1,
+            jnp.sum(from_up, axis=1, keepdims=True),
+            pltpu.roll(flat, depth - 1, 1),
+        ).reshape(values.shape)
         dn_x = fields[at, :, 7 : 7 + width, :]
         up_x = fields[at, :, 9 : 9 + width, :]
         coupled = tops[at][partner[0]] + tops[at][partner[1]]
         return up_x, dn_x, up_y, dn_y, coupled
 
-    pl.semaphore_wait(barrier, n_row - 1 + n_col - 1)
+    pl.semaphore_wait(barrier, n_row - 1 + 2)
     start_exchange(0, conduct, vent)
 
     @pl.loop(1, n_row)
     def _(i):
         remote(info.at[row], info.at[row], info_s, info_r, (peer(i, row, n_row), col)).start()
 
+    for copy in loads[2:]:
+        copy.wait()
+
     @pl.loop(0, vectors)
     def _(a):
-        zf[pl.ds(a * lines, lines), :] = basis_ref[a].astype(F32)
-
-    pad = width * vectors
-    zk[0:pad, :] = jnp.zeros((pad, depth), F32)
-    zk[pad + lines * vectors :, :] = jnp.zeros((pad, depth), F32)
+        zf[pl.ds(a * PITCH, lines), :] = basis_ref[a].astype(F32)
+
+    zk[lines * vectors :, :] = jnp.zeros((width * vectors, depth), F32)
 
     def line(k):
-        return pl.ds(pad + k * vectors, vectors)
-
-    @pl.loop(0, lines)
-    def _(k):
-        block = zf[pl.ds(k, vectors, stride=lines), :]
+        return pl.ds(k * vectors, vectors)
+
+    basis_lane = lax.broadcasted_iota(jnp.int32, (vectors, depth), 1)
+
+    def turn(k, sides):
+        block = zf[pl.ds(k, vectors, stride=PITCH), :]
         zk[line(k), :] = block
         zr[:, pl.ds(pl.multiple_of(k * depth, depth), depth)] = block.astype(BF16)
+        sides = jnp.where(basis_lane == k, block[:, 0:1], sides)
+        return jnp.where(basis_lane == lines + k, block[:, depth - 1 : depth], sides)
+
+    yb[...] = lax.fori_loop(0, lines, turn, jnp.zeros((vectors, depth), F32))
 
     def cells(k):
         return pl.ds(pl.multiple_of(k * depth, depth), depth)
@@ -257,14 +282,23 @@
         total = lax.fori_loop(0, lines, step, jnp.zeros((vectors, depth), F32), unroll=8)
         return jnp.sum(total, axis=1, keepdims=True)
 
-    def expand(coarse):
-        wide[...] = jnp.broadcast_to(coarse, wide.shape)
-
-        def step(a, total):
-            return total + zf[pl.ds(a * lines, lines), :] * wide[pl.ds(a, 1), :]
-
-        total = lax.fori_loop(0, vectors, step, jnp.zeros((lines, depth), F32), unroll=8)
-        return total.reshape(layers, width, depth)
+    def expand(at, coarse):
+        spread = jnp.broadcast_to(coarse, wide.shape)
+        wide[...] = spread
+        send_sides(at, jnp.sum(spread * yb[...], axis=0, keepdims=True))
+
+        def part(first, count):
+            def step(a, total):
+                return total + zf[pl.ds(a * PITCH + first, count), :] * wide[pl.ds(a, 1), :]
+
+            return lax.fori_loop(0, vectors, step, jnp.zeros((count, depth), F32), unroll=8)
+
+        top = part(top_line, width)
+        send_top(at, vent * top)
+        rest = part(0, top_line)
+        total = jnp.concatenate([rest, top], axis=0).reshape(layers, width, depth)
+        send_lines(at, total)
+        return total
 
     square_row = lax.broadcasted_iota(jnp.int32, (vectors, vectors), 0)
     square_col = lax.broadcasted_iota(jnp.int32, (vectors, vectors), 1)
@@ -276,30 +310,25 @@
     rhs = rhs_ref[...]
     first_side = project(rhs)
 
-    near = finish_exchange(0, conduct)
-    none = jnp.zeros((1, width, depth), F32)
-    up_z = jnp.concatenate([harmonic(conduct[:-1], conduct[1:]), none], axis=0)
-    dn_z = jnp.concatenate([none, up_z[:-1]], axis=0)
     x_id = lax.broadcasted_iota(jnp.int32, conduct.shape, 1)
     y_id = lax.broadcasted_iota(jnp.int32, conduct.shape, 2)
     x_last, x_first = x_id == width - 1, x_id == 0
     y_last, y_first = y_id == depth - 1, y_id == 0
-    up_x = jnp.where(x_last & (row == n_row - 1), 0.0, harmonic(conduct, near[0]))
-    dn_x = jnp.where(x_first & (row == 0), 0.0, harmonic(conduct, near[1]))
-    up_y = jnp.where(y_last & (col == n_col - 1), 0.0, harmonic(conduct, near[2]))
-    dn_y = jnp.where(y_first & (col == 0), 0.0, harmonic(conduct, near[3]))
-    diagonal = heat + up_z + dn_z + up_x + dn_x + up_y + dn_y
-    diagonal = jnp.concatenate(
-        [diagonal[:-1], (diagonal[-1] + vent * near[4])[None]], axis=0
-    )
-
-    local = (
-        diagonal, up_z, dn_z,
-        jnp.where(x_last, 0.0, up_x), jnp.where(x_first, 0.0, dn_x),
-        jnp.where(y_last, 0.0, up_y), jnp.where(y_first, 0.0, dn_y),
-    )
-    for c in range(7):
-        coef[c] = local[c].reshape(lines, depth)
+    none = jnp.zeros((1, width, depth), F32)
+    up_z = jnp.concatenate([harmonic(conduct[:-1], conduct[1:]), none], axis=0)
+    dn_z = jnp.concatenate([none, up_z[:-1]], axis=0)
+    in_up_x = jnp.where(x_last, 0.0, harmonic(conduct, pltpu.roll(conduct, width - 1, 1)))
+    in_dn_x = jnp.where(x_first, 0.0, pltpu.roll(in_up_x, 1, 1))
+    in_up_y = jnp.where(y_last, 0.0, harmonic(conduct, pltpu.roll(conduct, depth - 1, 2)))
+    in_dn_y = jnp.where(y_first, 0.0, pltpu.roll(in_up_y, 1, 2))
+    inside = heat + up_z + dn_z + in_up_x + in_dn_x + in_up_y + in_dn_y
+    for c, part in enumerate((0.5 * inside, up_z, in_up_x, in_up_y)):
+        coef[c] = part.reshape(lines, depth)
+
+    def keep(rows, where):
+        high, low = split(rows)
+        az[0:vectors, where] = high
+        az[vectors : 2 * vectors, where] = low
 
     @pl.loop(0, lines)
     def _(k):
@@ -308,16 +337,42 @@
         def at(c):
             return coef[c, pl.ds(k, 1), :]
 
-        applied = at(0) * own
-        applied = applied - at(1) * zk[line(k + width), :] - at(2) * zk[line(k - width), :]
-        applied = applied - at(3) * zk[line(k + 1), :] - at(4) * zk[line(k - 1), :]
-        applied = applied - at(5) * pltpu.roll(own, depth - 1, 1) - at(6) * pltpu.roll(own, 1, 1)
-        high, low = split(applied)
-        az[0:vectors, cells(k)] = high
-        az[vectors : 2 * vectors, cells(k)] = low
-
-    both = dot_t(az[...], zr[...])
-    own_block = both[:vectors] + both[vectors:]
+        applied = at(0) * own - at(1) * zk[line(k + width), :]
+        applied = applied - at(2) * zk[line(k + 1), :] - at(3) * pltpu.roll(own, depth - 1, 1)
+        keep(applied, cells(k))
+
+    half = dot_t(az[...], zr[...])
+    half = half[:vectors] + half[vectors:]
+    own_block = half + half.T
+
+    near = finish_exchange(0, conduct)
+    out_up_x = jnp.where(x_last & (row < n_row - 1), harmonic(conduct, near[0]), 0.0)
+    out_dn_x = jnp.where(x_first & (row > 0), harmonic(conduct, near[1]), 0.0)
+    out_up_y = jnp.where(y_last & (col < n_col - 1), harmonic(conduct, near[2]), 0.0)
+    out_dn_y = jnp.where(y_first & (col > 0), harmonic(conduct, near[3]), 0.0)
+    up_x, dn_x = in_up_x + out_up_x, in_dn_x + out_dn_x
+    up_y, dn_y = in_up_y + out_up_y, in_dn_y + out_dn_y
+    outside = jnp.concatenate(
+        [(out_up_x + out_dn_x)[:-1], (out_up_x + out_dn_x)[-1:] + (vent * near[4])[None]], axis=0
+    )
+    diagonal = inside + outside + out_up_y + out_dn_y
+
+    outer = [z * width + x for z in range(layers - 1) for x in (0, width - 1)]
+    outer += list(range(top_line, lines))
+    coef[4] = outside.reshape(lines, depth)
+    for i, k in enumerate(outer):
+        there = pl.ds(i * depth, depth)
+        keep(coef[4, k : k + 1, :] * zk[line(k), :], there)
+        zo[:, there] = zr[:, cells(k)]
+    side_gain = pack_sides(
+        out_dn_y.reshape(lines, depth)[:, 0:1], out_up_y.reshape(lines, depth)[:, depth - 1 : depth]
+    )
+    there = pl.ds(len(outer) * depth, depth)
+    keep(side_gain * yb[...], there)
+    zo[:, there] = yb[...].astype(BF16)
+    size = (len(outer) + 1) * depth
+    extra = dot_t(az[:, :size], zo[...])
+    own_block = own_block + extra[:vectors] + extra[vectors:]
     inv_ref[...] = inverse(own_block)
 
     def apply_start(at, values):
@@ -332,17 +387,21 @@
         result = result - up_x * near[0] - dn_x * near[1] - up_y * near[2] - dn_y * near[3]
         return jnp.concatenate([result[:-1], (result[-1] - vent * near[4])[None]], axis=0)
 
-    def apply(at, values, beside=None):
+    def apply(at, values, beside):
         apply_start(at, values)
-        if beside is not None:
-            beside()
+        beside()
         return apply_finish(at, values)
 
+    def apply_coarse(at, coarse, beside):
+        values = expand(at, coarse)
+        beside()
+        return values, apply_finish(at, values)
+
     def correct(at, right_side, besides):
-        first = expand(solve(right_side))
-        first_image = apply(at, first, besides[0])
-        second = expand(solve(right_side - project(first_image)))
-        second_image = apply(at + 1, second, besides[1])
+        first, first_image = apply_coarse(at, solve(right_side), besides[0])
+        second, second_image = apply_coarse(
+            at + 1, solve(right_side - project(first_image)), besides[1]
+        )
         return first + second, first_image + second_image
 
     def faces():
@@ -357,15 +416,26 @@
             wide_faces[side] = both[:vectors] + both[vectors:]
 
     wide_faces = [None, None]
-
-    def plenum():
+    third = n_row // 3
+
+    def nothing():
+        pass
+
+    def begin():
+        faces()
+        plenum_start()
+        plenum(0, third)
+
+    def plenum_start():
         wait_bytes(info.at[pl.ds(0, n_row - 1)], info_r)
         wait_bytes(pa.at[pl.ds(0, n_row - 1)], pa_r)
         first = top_line + row * share
         pa[row] = zr[:, pl.ds(pl.multiple_of(first * depth, depth), share * depth)]
 
-        @pl.loop(0, n_row)
-        def _(s):
+    def plenum(first, last):
+        @pl.loop(first, last)
+        def _(offset):
+            s = peer(offset, row, n_row)
             own = pa[s]
             total = None
             for i in range(share):
@@ -387,12 +457,13 @@
                 total = part if total is None else total + part
             pb[s] = total
 
-        @pl.loop(1, n_row)
-        def _(i):
-            target = peer(i, row, n_row)
-            remote(pb.at[target], pc.at[row], pc_s, pc_r, (target, col)).start()
-
-        pc[row] = pb[row]
+            @pl.when(offset > 0)
+            def _():
+                remote(pb.at[s], pc.at[row], pc_s, pc_r, (s, col)).start()
+
+            @pl.when(offset == 0)
+            def _():
+                pc[row] = pb[s]
 
     def finish_blocks():
         wait_bytes(pc.at[pl.ds(0, n_row - 1)], pc_r)
@@ -413,13 +484,15 @@
                 value = value + jnp.where(hit, 1.0, 0.0) * part
             e_ref[q] = value
 
-    iterate, image = correct(1, first_side, (faces, None))
+    iterate, image = correct(
+        1, first_side, (begin, lambda: plenum(third, 2 * third))
+    )
     defect = rhs - image
-    turned = apply(3, defect)
-    shift, image = correct(4, project(turned), (plenum, None))
+    turned = apply(3, defect, lambda: plenum(2 * third, n_row))
+    shift, image = correct(4, project(turned), (nothing, nothing))
     direction, stepped = defect - shift, turned - image
-    turned = apply(6, stepped)
-    shift, image = correct(7, project(turned), (None, finish_blocks))
+    turned = apply(6, stepped, finish_blocks)
+    shift, image = correct(7, project(turned), (nothing, nothing))
     slanted, slanted_image = stepped - shift, turned - image
 
     def lanes_of(left, right):
@@ -467,7 +540,7 @@
     )
 
     for at in range(ROUNDS):
-        for copy in side_copies(at):
+        for copy in x_copies(at) + y_copies(at):
             copy.wait_send()
         wait_bytes(tops[at].at[pl.ds(0, n_row - 1)], top_s.at[at])
 
@@ -485,27 +558,33 @@
     vectors = basis.shape[0]
     lines, share = layers * width, width // n_row
     smem, vmem = pl.BlockSpec(memory_space=pltpu.SMEM), pl.BlockSpec(memory_space=pltpu.VMEM)
+    hbm = pl.BlockSpec(memory_space=pltpu.HBM)
+    outer = 2 * (layers - 1) + width
     dma = pltpu.SemaphoreType.DMA
     scratch = [
+        pltpu.VMEM(rhs.shape, F32), pltpu.VMEM(material.shape, jnp.int32),
+        pltpu.VMEM(vent.shape, F32), pltpu.VMEM((vectors, lines, depth), BF16),
         pltpu.VMEM((ROUNDS, layers, width + 16, depth), F32),
         pltpu.VMEM((ROUNDS, 8, LANES), F32),
         pltpu.VMEM((ROUNDS, 2, 8, LANES), F32),
         pltpu.VMEM((n_row, 8, LANES), F32),
-        pltpu.VMEM((vectors * lines, depth), F32),
-        pltpu.VMEM((vectors * (lines + 2 * width), depth), F32),
+        pltpu.VMEM((vectors * PITCH, depth), F32),
+        pltpu.VMEM((vectors * (lines + width), depth), F32),
         pltpu.VMEM((vectors, lines * depth), BF16),
+        pltpu.VMEM((vectors, depth), F32),
         pltpu.VMEM((2 * vectors, lines * depth), BF16),
         pltpu.VMEM((2, vectors, layers * depth), BF16),
         pltpu.VMEM((n_row, vectors, share * depth), BF16),
         pltpu.VMEM((n_row, vectors, 2 * vectors), F32),
         pltpu.VMEM((n_row, vectors, 2 * vectors), F32),
-        pltpu.VMEM((7, lines, depth), F32),
+        pltpu.VMEM((5, lines, depth), F32),
+        pltpu.VMEM((vectors, (outer + 1) * depth), BF16),
         pltpu.VMEM((lines, depth), F32),
         pltpu.VMEM((vectors, depth), F32),
         pltpu.VMEM((vectors, vectors), F32),
         pltpu.VMEM((n_row, 8, LANES), F32),
         pltpu.VMEM((n_col, 8, LANES), F32),
-        dma((ROUNDS,)), dma((ROUNDS,)), dma((ROUNDS, 2)), dma((ROUNDS, 2)),
+        dma((4,)), dma((ROUNDS,)), dma((ROUNDS,)), dma((ROUNDS, 2)), dma((ROUNDS, 2)),
         dma((ROUNDS, 2)), dma((ROUNDS, 2)), dma, dma, dma((2, layers)), dma((2, layers)),
         dma, dma, dma, dma, dma, dma, dma, dma,
         *[pltpu.VMEM((n_row, width, depth), F32) for _ in range(ROUNDS)],
@@ -517,7 +596,7 @@
             jax.ShapeDtypeStruct(rhs.shape, F32),
             jax.ShapeDtypeStruct((n_row, vectors, vectors), F32),
         ),
-        in_specs=[smem, smem, smem, vmem, vmem, vmem, vmem],
+        in_specs=[smem, smem, smem, hbm, hbm, hbm, hbm],
         out_specs=(vmem, vmem, vmem),
         scratch_shapes=scratch,
         compiler_params=pltpu.CompilerParams(

time: 88.9 us -> 85.7 us (0.964)
  Pallas kernels: 81.8 us -> 78.6 us
    pallas_call x1, Pallas kernels: 81.8 us -> 78.6 us  [body(): pl.pallas_call(functools.partial(kernel, n_row, n_col), out_shape=(jax.Sh...]
where the time goes in v2:
time: 85.7 us; the launch traced here: 85.4 us
  Pallas kernels  78.6 us (92%)
  local copies, waits for them, and re-layouts  6.12 us (7%)
    pallas_call x1, Pallas kernels, body(): pl.pallas_call(functools.partial(kernel, n_row, n_col), out_shape=(jax.Sh...  78.6 us
    unnamed x17, local copies, waits for them, and re-layouts  6.12 us

profile of v2, /device:TPU:1, one launch (start us, length us, event | category | flops | bytes accessed | tf_op | source)
XLA Modules:
  0.0 85.4 jit_solution(5736179921514998201)
XLA Ops:
  0.6 0.0 copy-start.4
  0.6 0.0 copy-start.5
  0.7 0.0 copy-start.6
  0.7 0.6 copy-done.4
  1.3 0.0 copy-done.5
  1.3 0.0 copy-done.6
  1.3 0.0 copy-start
  1.3 1.2 %copy-done = bf16[64,4,16,128]{3,2,1,0:T(8,128)(2,1)S(1)} copy-done((bf16[64,4,16,128]{3,2,1,0:T(8,128)(2,1)S(1)}, bf16[64,4,16,128]{3,2,1,0:T(8,128)(2,1)}, u32[]{:S(2)}) %copy-start) | copy-done | bytes 1048600
  2.5 0.0 copy-start.1
  2.5 0.8 copy-done.1
  3.3 0.0 copy-start.2
  3.3 0.8 copy-done.2
  4.1 0.0 copy-start.3
  4.1 0.7 copy-done.3
  4.8 78.6 %deflated_cg.1 = (f32[4,16,128]{2,1,0:T(8,128)S(1)}, f32[4,16,128]{2,1,0:T(8,128)S(1)}, f32[16,64,64]{2,1,0:T(8,128)S(1)}) custom-call(f32[8]{0:T(128)S(1)} %copy-done.4, f32[8]{0:T(128)S(1)} %copy-done.5, s32[2]{0:T(128)S(1)} %bitcast.5, f32[4,16,128]{2,1,0:T(8,128)S(1)} %copy-done.1, s32[4,16,128]{2,1,0:T(8,128)S(1)} %copy-done.2, ...), custom_call_target="tpu_custom_call" | custom-call | tf_op jit(solution)/shard_map/deflated_cg/pallas_call | solution.py:592
  83.4 0.6 copy.13
  84.0 0.6 copy.14
  84.6 0.8 copy.15
Async XLA Ops:
  0.6 0.7 copy-start.4
  0.6 0.7 copy-start.5
  0.7 0.7 copy-start.6
  1.3 1.2 %copy-start = (bf16[64,4,16,128]{3,2,1,0:T(8,128)(2,1)S(1)}, bf16[64,4,16,128]{3,2,1,0:T(8,128)(2,1)}, u32[]{:S(2)}) copy-start(bf16[64,4,16,128]{3,2,1,0:T(8,128)(2,1)} %param.13) | copy-start | bytes 3145732
  2.5 0.8 copy-start.1
  3.3 0.8 copy-start.2
  4.1 0.7 copy-start.3

commit v3 on v2

--- a/solution.py
+++ b/solution.py
@@ -13,6 +13,7 @@
 PIVOTS = 4
 ROUNDS = 9
 PITCH = 72
+COARSE_ROUNDS = (4, 7)
 
 
 def harmonic(left_side, right_side):
@@ -51,17 +52,22 @@
             for j in ids
         ]
         work = jnp.where(inside, 0.0, work)
-        for p in ids:
-            scale = 1.0 / pivot[p][p]
-            rows[p] = rows[p] * scale
-            for j in range(p + 1, PIVOTS):
-                pivot[p][j] = pivot[p][j] * scale
+        for p in range(0, PIVOTS, 2):
+            (a, b), (c, d) = (pivot[p + i][p : p + 2] for i in range(2))
+            scale = 1.0 / (a * d - b * c)
+            a, b, c, d = d * scale, -b * scale, -c * scale, a * scale
+            rows[p], rows[p + 1] = a * rows[p] + b * rows[p + 1], c * rows[p] + d * rows[p + 1]
+            for j in range(p + 2, PIVOTS):
+                first, second = pivot[p][j], pivot[p + 1][j]
+                pivot[p][j], pivot[p + 1][j] = a * first + b * second, c * first + d * second
             for i in ids:
-                if i != p:
-                    factor = pivot[i][p]
-                    rows[i] = rows[i] - factor * rows[p]
-                    for j in range(p + 1, PIVOTS):
-                        pivot[i][j] = pivot[i][j] - factor * pivot[p][j]
+                if i not in (p, p + 1):
+                    first, second = pivot[i][p], pivot[i][p + 1]
+                    rows[i] = rows[i] - (first * rows[p] + second * rows[p + 1])
+                    for j in range(p + 2, PIVOTS):
+                        pivot[i][j] = pivot[i][j] - (
+                            first * pivot[p][j] + second * pivot[p + 1][j]
+                        )
         for j in ids:
             work = work - columns[j] * rows[j]
     return work[:, n:]
@@ -72,11 +78,12 @@
     cap_ref, con_ref, par_ref, rhs_hbm, mat_hbm, vent_hbm, basis_hbm,
     x_ref, r_ref, e_ref,
     rhs_ref, mat_ref, vent_ref, basis_ref,
-    fields, ysend, yrecv, info, zf, zk, zr, yb, az, xb, pa, pb, pc, coef, zo, work, wide, inv_ref,
+    fields, ysend, yrecv, info, zf, zk, zr, yb, ybs, ybr, eb, ysv, yrv, az, xb, pa, pb, pc, coef, zo, work, wide, inv_ref,
     red_row, red_col, load,
-    top_s, top_r, x_s, x_r, y_s, y_r, info_s, info_r, xb_s, xb_r, pa_s, pa_r, pc_s, pc_r,
-    rr_s, rr_r, rc_s, rc_r, *tops,
+    top_s, top_r, x_s, x_r, y_s, y_r, info_s, info_r, yb_s, yb_r, xb_s, xb_r, pa_s, pa_r, pc_s, pc_r,
+    rr_s, rr_r, rc_s, rc_r, *more,
 ):
+    tops, coarse_rows = more[:ROUNDS], dict(zip(COARSE_ROUNDS, more[ROUNDS:]))
     layers, width, depth = rhs_ref.shape
     vectors = basis_ref.shape[0]
     lines = layers * width
@@ -85,10 +92,21 @@
     row_up, row_dn = lax.rem(row + 1, n_row), lax.rem(row + n_row - 1, n_row)
     col_up, col_dn = lax.rem(col + 1, n_col), lax.rem(col + n_col - 1, n_col)
 
-    order = sorted(range(1, n_row), key=lambda i: min(i, n_row - i), reverse=True)
+    count_x = n_row // 4
+    steps = [(dx, dy, dc) for dx in range(count_x) for dy in range(2) for dc in range(2)]
+    steps = sorted(steps[1:], key=lambda s: (min(s[0], count_x - s[0]) + s[1], s), reverse=True)
 
     def peer(i, me, count):
         return lax.rem(me + i, count)
+
+    def row_peers():
+        x, rest = row // 4, lax.rem(row, 4)
+        for dx, dy, dc in steps:
+            yield (
+                lax.rem(x + dx, count_x) * 4
+                + lax.rem(rest // 2 + dy, 2) * 2
+                + lax.rem(lax.rem(rest, 2) + dc, 2)
+            )
 
     def remote(src, dst, send, recv, target):
         return pltpu.make_async_remote_copy(
@@ -152,10 +170,9 @@
 
     def send_top(at, top):
         tops[at][row] = top
-        for i in order:
+        for other in row_peers():
             remote(
-                tops[at].at[row], tops[at].at[row], top_s.at[at], top_r.at[at],
-                (peer(i, row, n_row), col),
+                tops[at].at[row], tops[at].at[row], top_s.at[at], top_r.at[at], (other, col)
             ).start()
 
     def send_lines(at, values):
@@ -238,6 +255,11 @@
         return jnp.where(basis_lane == lines + k, block[:, depth - 1 : depth], sides)
 
     yb[...] = lax.fori_loop(0, lines, turn, jnp.zeros((vectors, depth), F32))
+    ybs[...] = yb[...].astype(BF16)
+    side_basis = (
+        remote(ybs, ybr.at[0], yb_s.at[0], yb_r.at[0], (row, col_up)),
+        remote(ybs, ybr.at[1], yb_s.at[1], yb_r.at[1], (row, col_dn)),
+    )
 
     def cells(k):
         return pl.ds(pl.multiple_of(k * depth, depth), depth)
@@ -261,7 +283,7 @@
         return copies
 
     top_line = (layers - 1) * width
-    for copy in face_copies():
+    for copy in face_copies() + list(side_basis):
         copy.start()
 
     @pl.loop(1, n_row)
@@ -404,9 +426,56 @@
         )
         return first + second, first_image + second_image
 
+    def coarse_copies(at):
+        i = COARSE_ROUNDS.index(at)
+        return (
+            remote(ysv.at[i], yrv.at[i, 0], y_s.at[at, 0], y_r.at[at, 0], (row, col_up)),
+            remote(ysv.at[i], yrv.at[i, 1], y_s.at[at, 1], y_r.at[at, 1], (row, col_dn)),
+        )
+
+    def correct_by_blocks(at, right_side, besides):
+        coarse = solve(right_side)
+        i, held = COARSE_ROUNDS.index(at), coarse_rows[at]
+        packed = jnp.broadcast_to(pack_sides(coarse, coarse), (8, LANES))
+        ysv[i] = packed
+        held[row] = packed
+        for copy in coarse_copies(at):
+            copy.start()
+        mine = held.at[row, pl.ds(0, 1)]
+        for other in row_peers():
+            remote(mine, mine, top_s.at[at], top_r.at[at], (other, col)).start()
+        besides[0]()
+        for copy in coarse_copies(at):
+            copy.wait_recv()
+        wait_bytes(held.at[pl.ds(0, n_row - 1), pl.ds(0, 1)], top_r.at[at])
+        first_half = lax.broadcasted_iota(jnp.int32, (1, LANES), 1) < vectors
+        pairs = (
+            (held[row_dn, 0:1], held[row_up, 0:1]),
+            (yrv[i, 0, 0:1], yrv[i, 1, 0:1]),
+            (held[partner[0], 0:1], held[partner[1], 0:1]),
+        )
+        total = jnp.zeros((vectors, 2 * vectors), F32)
+        for pair, (left, right) in enumerate(pairs):
+            total = total + eb[pair] * jnp.where(first_half, left, right)
+        coarse = coarse - solve(jnp.sum(total, axis=1, keepdims=True))
+        return apply_coarse(at + 1, coarse, besides[1])
+
     def faces():
-        for copy in face_copies():
+        for copy in face_copies() + list(side_basis):
             copy.wait_recv()
+        halves = [pltpu.roll(ybr[side].astype(F32), depth - lines, 1) for side in range(2)]
+        high, low = split(side_gain * yb[...])
+        both = dot_t(
+            jnp.concatenate([high, low], axis=0),
+            jnp.concatenate(
+                [
+                    jnp.where(basis_lane < lines, halves[0], 0.0),
+                    jnp.where(basis_lane < lines, 0.0, halves[1]),
+                ],
+                axis=0,
+            ).astype(BF16),
+        )
+        eb[1] = -(both[:vectors] + both[vectors:])
         for side, at, coefficient in ((0, 0, dn_x), (1, width - 1, up_x)):
             terms = [
                 zk[line(z * width + at), :] * coefficient[z, at : at + 1, :] for z in range(layers)
@@ -416,6 +485,14 @@
             wide_faces[side] = both[:vectors] + both[vectors:]
 
     wide_faces = [None, None]
+
+    def couplings():
+        eb[0] = -jnp.concatenate(wide_faces, axis=1)
+        wait_bytes(pc.at[pl.ds(0, n_row - 1)], pc_r)
+        eb[2] = -lax.fori_loop(
+            0, n_row, lambda i, t: t + pc[i], jnp.zeros((vectors, 2 * vectors), F32)
+        )
+
     third = n_row // 3
 
     def nothing():
@@ -466,14 +543,10 @@
                 pc[row] = pb[s]
 
     def finish_blocks():
-        wait_bytes(pc.at[pl.ds(0, n_row - 1)], pc_r)
-        total = lax.fori_loop(
-            0, n_row, lambda i, t: t + pc[i], jnp.zeros((vectors, 2 * vectors), F32)
-        )
         scale = 1.0 / (lines * depth)
         parts = (
-            own_block * scale, wide_faces[0] * -scale, wide_faces[1] * -scale,
-            total[:, :vectors] * -scale, total[:, vectors:] * -scale,
+            own_block * scale, eb[0, :, :vectors] * scale, eb[0, :, vectors:] * scale,
+            eb[2, :, :vectors] * scale, eb[2, :, vectors:] * scale,
         )
 
         @pl.loop(0, n_row)
@@ -489,10 +562,10 @@
     )
     defect = rhs - image
     turned = apply(3, defect, lambda: plenum(2 * third, n_row))
-    shift, image = correct(4, project(turned), (nothing, nothing))
+    shift, image = correct_by_blocks(4, project(turned), (couplings, nothing))
     direction, stepped = defect - shift, turned - image
     turned = apply(6, stepped, finish_blocks)
-    shift, image = correct(7, project(turned), (nothing, nothing))
+    shift, image = correct_by_blocks(7, project(turned), (nothing, nothing))
     slanted, slanted_image = stepped - shift, turned - image
 
     def lanes_of(left, right):
@@ -502,49 +575,55 @@
         lanes_of(defect, defect), lanes_of(direction, stepped), lanes_of(defect, stepped),
         lanes_of(stepped, stepped), lanes_of(slanted, stepped), lanes_of(slanted, slanted_image),
     ]
-    red_row[row] = jnp.concatenate(sums + [jnp.zeros((2, depth), F32)], axis=0)
-
-    @pl.loop(1, n_row)
-    def _(i):
-        remote(red_row.at[row], red_row.at[row], rr_s, rr_r, (peer(i, row, n_row), col)).start()
-
+    sums = jnp.concatenate(sums + [jnp.zeros((2, depth), F32)], axis=0)
+    scalar_at = lax.broadcasted_iota(jnp.int32, (8, LANES), 0) == lax.broadcasted_iota(
+        jnp.int32, (8, LANES), 1
+    )
+    sums = jnp.where(scalar_at, jnp.sum(sums, axis=1, keepdims=True), 0.0)
+    red_row[row] = jnp.sum(sums, axis=0, keepdims=True)
+    for other in row_peers():
+        remote(red_row.at[row], red_row.at[row], rr_s, rr_r, (other, col)).start()
     wait_bytes(red_row.at[pl.ds(0, n_row - 1)], rr_r)
     red_col[col] = jnp.sum(red_row[...], axis=0)
-
-    @pl.loop(1, n_col)
-    def _(i):
+    ring = n_col // 2
+    for i in sorted(range(1, n_col), key=lambda i: min(i % ring, ring - i % ring), reverse=True):
         remote(red_col.at[col], red_col.at[col], rc_s, rc_r, (row, peer(i, col, n_col))).start()
-
     wait_bytes(red_col.at[pl.ds(0, n_col - 1)], rc_r)
-    scalars = jnp.sum(jnp.sum(red_col[...], axis=0), axis=1, keepdims=True)
+    scalars = jnp.where(scalar_at, jnp.sum(red_col[...], axis=0), 0.0)
+    scalars = jnp.sum(scalars, axis=1, keepdims=True)
     norm, curve, cross, square, mixed, slant = [scalars[i : i + 1, :] for i in range(6)]
     alpha = norm / curve
     after = norm - 2.0 * alpha * cross + alpha * alpha * square
-    more = 1.0 + after / norm
-    curve = more * more * curve - 2.0 * more * alpha * mixed + alpha * alpha * slant
+    gain = 1.0 + after / norm
+    curve = gain * gain * curve - 2.0 * gain * alpha * mixed + alpha * alpha * slant
     last = after / curve
 
     def scaled(factor, values):
         return jnp.broadcast_to(factor, values.shape) * values
 
-    alpha, more, last = alpha[None], more[None], last[None]
+    alpha, gain, last = alpha[None], gain[None], last[None]
     x_ref[...] = (
         iterate
         + scaled(alpha, direction)
-        + scaled(last, scaled(more, direction) - scaled(alpha, slanted))
+        + scaled(last, scaled(gain, direction) - scaled(alpha, slanted))
     )
     r_ref[...] = (
         defect
         - scaled(alpha, stepped)
-        - scaled(last, scaled(more, stepped) - scaled(alpha, slanted_image))
+        - scaled(last, scaled(gain, stepped) - scaled(alpha, slanted_image))
     )
 
     for at in range(ROUNDS):
-        for copy in x_copies(at) + y_copies(at):
-            copy.wait_send()
-        wait_bytes(tops[at].at[pl.ds(0, n_row - 1)], top_s.at[at])
-
-    for copy in face_copies():
+        if at in COARSE_ROUNDS:
+            for copy in coarse_copies(at):
+                copy.wait_send()
+            wait_bytes(coarse_rows[at].at[pl.ds(0, n_row - 1), pl.ds(0, 1)], top_s.at[at])
+        else:
+            for copy in x_copies(at) + y_copies(at):
+                copy.wait_send()
+            wait_bytes(tops[at].at[pl.ds(0, n_row - 1)], top_s.at[at])
+
+    for copy in face_copies() + list(side_basis):
         copy.wait_send()
     wait_bytes(info.at[pl.ds(0, n_row - 1)], info_s)
     wait_bytes(pa.at[pl.ds(0, n_row - 1)], pa_s)
@@ -572,6 +651,11 @@
         pltpu.VMEM((vectors * (lines + width), depth), F32),
         pltpu.VMEM((vectors, lines * depth), BF16),
         pltpu.VMEM((vectors, depth), F32),
+        pltpu.VMEM((vectors, depth), BF16),
+        pltpu.VMEM((2, vectors, depth), BF16),
+        pltpu.VMEM((3, vectors, 2 * vectors), F32),
+        pltpu.VMEM((len(COARSE_ROUNDS), 8, LANES), F32),
+        pltpu.VMEM((len(COARSE_ROUNDS), 2, 8, LANES), F32),
         pltpu.VMEM((2 * vectors, lines * depth), BF16),
         pltpu.VMEM((2, vectors, layers * depth), BF16),
         pltpu.VMEM((n_row, vectors, share * depth), BF16),
@@ -582,12 +666,13 @@
         pltpu.VMEM((lines, depth), F32),
         pltpu.VMEM((vectors, depth), F32),
         pltpu.VMEM((vectors, vectors), F32),
-        pltpu.VMEM((n_row, 8, LANES), F32),
-        pltpu.VMEM((n_col, 8, LANES), F32),
+        pltpu.VMEM((n_row, 1, LANES), F32),
+        pltpu.VMEM((n_col, 1, LANES), F32),
         dma((4,)), dma((ROUNDS,)), dma((ROUNDS,)), dma((ROUNDS, 2)), dma((ROUNDS, 2)),
-        dma((ROUNDS, 2)), dma((ROUNDS, 2)), dma, dma, dma((2, layers)), dma((2, layers)),
+        dma((ROUNDS, 2)), dma((ROUNDS, 2)), dma, dma, dma((2,)), dma((2,)), dma((2, layers)), dma((2, layers)),
         dma, dma, dma, dma, dma, dma, dma, dma,
         *[pltpu.VMEM((n_row, width, depth), F32) for _ in range(ROUNDS)],
+        *[pltpu.VMEM((n_row, 8, LANES), F32) for _ in COARSE_ROUNDS],
     ]
     iterate, defect, blocks = pl.pallas_call(
         functools.partial(kernel, n_row, n_col),
@@ -600,7 +685,7 @@
         out_specs=(vmem, vmem, vmem),
         scratch_shapes=scratch,
         compiler_params=pltpu.CompilerParams(
-            collective_id=0, has_side_effects=True, vmem_limit_bytes=48 * 1024 * 1024
+            collective_id=0, has_side_effects=True, vmem_limit_bytes=67043328
         ),
         name="deflated_cg",
     )(

time: 85.7 us -> 82.5 us (0.963)
  local copies, waits for them, and re-layouts: 6.12 us -> 3.88 us
    unnamed x17 -> x5, local copies, waits for them, and re-layouts: 6.12 us -> 3.88 us
    pallas_call x1, Pallas kernels: 78.6 us -> 77.8 us  [body(): pl.pallas_call(functools.partial(kernel, n_row, n_col), out_shape=(jax.Sh...]
where the time goes in v3:
time: 82.5 us; the launch traced here: 82.3 us
  Pallas kernels  77.8 us (94%)
  local copies, waits for them, and re-layouts  3.88 us (5%)
    pallas_call x1, Pallas kernels, body(): pl.pallas_call(functools.partial(kernel, n_row, n_col), out_shape=(jax.Sh...  77.8 us
    unnamed x5, local copies, waits for them, and re-layouts  3.88 us

profile of v3, /device:TPU:1, one launch (start us, length us, event | category | flops | bytes accessed | tf_op | source)
XLA Modules:
  0.0 82.3 jit_solution(4303126642930868721)
XLA Ops:
  0.6 77.8 %deflated_cg.1 = (f32[4,16,128]{2,1,0:T(8,128)}, f32[4,16,128]{2,1,0:T(8,128)}, f32[16,64,64]{2,1,0:T(8,128)}) custom-call(f32[8]{0:T(128)} %cap_ref.1, f32[8]{0:T(128)} %con_ref.1, s32[2]{0:T(128)} %bitcast.5, f32[4,16,128]{2,1,0:T(8,128)} %rhs_hbm.1, s32[4,16,128]{2,1,0:T(8,128)} %mat_hbm.1, f32[16,128]{1,0:T(8,128)} %vent_hbm.1, bf16[64,64,128]{2,1,0:T(8,128)(2,1)} %bitcast.3), custom_call_target="tpu_custom_call" | custom-call | tf_op jit(solution)/shard_map/deflated_cg/pallas_call | solution.py:677
  78.4 0.0 copy-start
  78.4 1.4 %copy.13 = f32[4,16,128]{2,1,0:T(8,128)} copy(f32[4,16,128]{2,1,0:T(8,128)} %get-tuple-element.12) | data formatting | bytes 65536
  79.8 0.0 copy-done
  79.8 0.6 copy.14
  80.4 1.9 %copy.15 = f32[1,1,16,64,64]{4,3,2,1,0:T(8,128)} copy(f32[1,1,16,64,64]{4,3,2,1,0:T(8,128)} %bitcast.4) | data formatting | bytes 524288
Async XLA Ops:
  78.4 1.4 %copy-start = (f32[4,16,128]{2,1,0:T(8,128)S(1)}, f32[4,16,128]{2,1,0:T(8,128)}, u32[]{:S(2)}) copy-start(f32[4,16,128]{2,1,0:T(8,128)} %get-tuple-element.13) | copy-start | bytes 98308

commit v4 on v3

--- a/solution.py
+++ b/solution.py
@@ -236,7 +236,7 @@
     for copy in loads[2:]:
         copy.wait()
 
-    @pl.loop(0, vectors)
+    @pl.loop(0, vectors, unroll=4)
     def _(a):
         zf[pl.ds(a * PITCH, lines), :] = basis_ref[a].astype(F32)
 
@@ -254,7 +254,7 @@
         sides = jnp.where(basis_lane == k, block[:, 0:1], sides)
         return jnp.where(basis_lane == lines + k, block[:, depth - 1 : depth], sides)
 
-    yb[...] = lax.fori_loop(0, lines, turn, jnp.zeros((vectors, depth), F32))
+    yb[...] = lax.fori_loop(0, lines, turn, jnp.zeros((vectors, depth), F32), unroll=8)
     ybs[...] = yb[...].astype(BF16)
     side_basis = (
         remote(ybs, ybr.at[0], yb_s.at[0], yb_r.at[0], (row, col_up)),
@@ -352,7 +352,7 @@
         az[0:vectors, where] = high
         az[vectors : 2 * vectors, where] = low
 
-    @pl.loop(0, lines)
+    @pl.loop(0, lines, unroll=4)
     def _(k):
         own = zk[line(k), :]
 

time: 82.5 us -> 75 us (0.909)
  Pallas kernels: 77.8 us -> 70.2 us
    pallas_call x1, Pallas kernels: 77.8 us -> 70.2 us  [body(): pl.pallas_call(functools.partial(kernel, n_row, n_col), out_shape=(jax.Sh...]
where the time goes in v4:
time: 75 us; the launch traced here: 74.7 us
  Pallas kernels  70.2 us (94%)
  local copies, waits for them, and re-layouts  3.88 us (5%)
    pallas_call x1, Pallas kernels, body(): pl.pallas_call(functools.partial(kernel, n_row, n_col), out_shape=(jax.Sh...  70.2 us
    unnamed x5, local copies, waits for them, and re-layouts  3.88 us

profile of v4, /device:TPU:1, one launch (start us, length us, event | category | flops | bytes accessed | tf_op | source)
XLA Modules:
  0.0 74.7 jit_solution(18407124665473944177)
XLA Ops:
  0.6 70.2 %deflated_cg.1 = (f32[4,16,128]{2,1,0:T(8,128)}, f32[4,16,128]{2,1,0:T(8,128)}, f32[16,64,64]{2,1,0:T(8,128)}) custom-call(f32[8]{0:T(128)} %cap_ref.1, f32[8]{0:T(128)} %con_ref.1, s32[2]{0:T(128)} %bitcast.5, f32[4,16,128]{2,1,0:T(8,128)} %rhs_hbm.1, s32[4,16,128]{2,1,0:T(8,128)} %mat_hbm.1, f32[16,128]{1,0:T(8,128)} %vent_hbm.1, bf16[64,64,128]{2,1,0:T(8,128)(2,1)} %bitcast.3), custom_call_target="tpu_custom_call" | custom-call | tf_op jit(solution)/shard_map/deflated_cg/pallas_call | solution.py:677
  70.9 0.0 copy-start
  70.9 1.4 %copy.13 = f32[4,16,128]{2,1,0:T(8,128)} copy(f32[4,16,128]{2,1,0:T(8,128)} %get-tuple-element.12) | data formatting | bytes 65536
  72.2 0.0 copy-done
  72.2 0.6 copy.14
  72.9 1.9 %copy.15 = f32[1,1,16,64,64]{4,3,2,1,0:T(8,128)} copy(f32[1,1,16,64,64]{4,3,2,1,0:T(8,128)} %bitcast.4) | data formatting | bytes 524288
Async XLA Ops:
  70.9 1.4 %copy-start = (f32[4,16,128]{2,1,0:T(8,128)S(1)}, f32[4,16,128]{2,1,0:T(8,128)}, u32[]{:S(2)}) copy-start(f32[4,16,128]{2,1,0:T(8,128)} %get-tuple-element.13) | copy-start | bytes 98308

commit v5 on v4

--- a/solution.py
+++ b/solution.py
@@ -13,7 +13,7 @@
 PIVOTS = 4
 ROUNDS = 9
 PITCH = 72
-COARSE_ROUNDS = (4, 7)
+COARSE_ROUNDS = (7,)
 
 
 def harmonic(left_side, right_side):
@@ -182,8 +182,8 @@
 
     def start_exchange(at, values, top):
         flat = values.reshape(lines, depth)
+        send_top(at, top)
         send_sides(at, pack_sides(flat[:, 0:1], flat[:, depth - 1 : depth]))
-        send_top(at, top)
         send_lines(at, values)
 
     def x_copies(at):
@@ -301,7 +301,7 @@
         def step(k, total):
             return total + zk[line(k), :] * work[pl.ds(k, 1), :]
 
-        total = lax.fori_loop(0, lines, step, jnp.zeros((vectors, depth), F32), unroll=8)
+        total = lax.fori_loop(0, lines, step, jnp.zeros((vectors, depth), F32), unroll=32)
         return jnp.sum(total, axis=1, keepdims=True)
 
     def expand(at, coarse):
@@ -313,7 +313,7 @@
             def step(a, total):
                 return total + zf[pl.ds(a * PITCH + first, count), :] * wide[pl.ds(a, 1), :]
 
-            return lax.fori_loop(0, vectors, step, jnp.zeros((count, depth), F32), unroll=8)
+            return lax.fori_loop(0, vectors, step, jnp.zeros((count, depth), F32), unroll=32)
 
         top = part(top_line, width)
         send_top(at, vent * top)
@@ -493,7 +493,7 @@
             0, n_row, lambda i, t: t + pc[i], jnp.zeros((vectors, 2 * vectors), F32)
         )
 
-    third = n_row // 3
+    cuts = [n_row * i // 5 for i in range(1, 5)]
 
     def nothing():
         pass
@@ -501,7 +501,7 @@
     def begin():
         faces()
         plenum_start()
-        plenum(0, third)
+        plenum(0, cuts[0])
 
     def plenum_start():
         wait_bytes(info.at[pl.ds(0, n_row - 1)], info_r)
@@ -558,14 +558,16 @@
             e_ref[q] = value
 
     iterate, image = correct(
-        1, first_side, (begin, lambda: plenum(third, 2 * third))
+        1, first_side, (begin, lambda: plenum(cuts[0], cuts[1]))
     )
     defect = rhs - image
-    turned = apply(3, defect, lambda: plenum(2 * third, n_row))
-    shift, image = correct_by_blocks(4, project(turned), (couplings, nothing))
+    turned = apply(3, defect, lambda: plenum(cuts[1], cuts[2]))
+    shift, image = correct(
+        4, project(turned), (lambda: plenum(cuts[2], cuts[3]), lambda: plenum(cuts[3], n_row))
+    )
     direction, stepped = defect - shift, turned - image
-    turned = apply(6, stepped, finish_blocks)
-    shift, image = correct_by_blocks(7, project(turned), (nothing, nothing))
+    turned = apply(6, stepped, couplings)
+    shift, image = correct_by_blocks(7, project(turned), (nothing, finish_blocks))
     slanted, slanted_image = stepped - shift, turned - image
 
     def lanes_of(left, right):
@@ -685,12 +687,17 @@
         out_specs=(vmem, vmem, vmem),
         scratch_shapes=scratch,
         compiler_params=pltpu.CompilerParams(
-            collective_id=0, has_side_effects=True, vmem_limit_bytes=67043328
+            collective_id=0, has_side_effects=True, vmem_limit_bytes=48 * 1024 * 1024
         ),
         name="deflated_cg",
     )(
-        capacity, conductivity, partners.reshape(-1), rhs, material, vent,
-        basis.reshape(vectors, lines, depth),
+        *[
+            pltpu.with_memory_space_constraint(array, pltpu.HBM)
+            for array in (
+                capacity, conductivity, partners.reshape(-1),
+                rhs, material, vent, basis.reshape(vectors, lines, depth),
+            )
+        ],
     )
     return iterate, defect, blocks[None, None]
 

time: 75 us -> 71 us (0.947)
  Pallas kernels: 70.2 us -> 68.2 us
  local copies, waits for them, and re-layouts: 3.88 us -> 2.02 us
    pallas_call x1, Pallas kernels: 70.2 us -> 68.2 us  [body(): pl.pallas_call(functools.partial(kernel, n_row, n_col), out_shape=(jax.Sh...]
    unnamed x5 -> x3, local copies, waits for them, and re-layouts: 3.88 us -> 2.02 us
where the time goes in v5:
time: 71 us; the launch traced here: 70.9 us
  Pallas kernels  68.2 us (96%)
  local copies, waits for them, and re-layouts  2.02 us (3%)
    pallas_call x1, Pallas kernels, body(): pl.pallas_call(functools.partial(kernel, n_row, n_col), out_shape=(jax.Sh...  68.2 us
    unnamed x3, local copies, waits for them, and re-layouts  2.02 us

profile of v5, /device:TPU:1, one launch (start us, length us, event | category | flops | bytes accessed | tf_op | source)
XLA Modules:
  0.0 70.9 jit_solution(13915149870158276906)
XLA Ops:
  0.6 68.2 %deflated_cg.1 = (f32[4,16,128]{2,1,0:T(8,128)S(1)}, f32[4,16,128]{2,1,0:T(8,128)S(1)}, f32[16,64,64]{2,1,0:T(8,128)S(1)}) custom-call(f32[8]{0:T(128)} %cap_ref.1, f32[8]{0:T(128)} %con_ref.1, s32[2]{0:T(128)} %bitcast.5, f32[4,16,128]{2,1,0:T(8,128)} %rhs_hbm.1, s32[4,16,128]{2,1,0:T(8,128)} %mat_hbm.1, f32[16,128]{1,0:T(8,128)} %vent_hbm.1, ...), custom_call_target="tpu_custom_call" | custom-call | tf_op jit(solution)/shard_map/deflated_cg/pallas_call | solution.py:679
  68.9 0.6 copy.13
  69.5 0.6 copy.14
  70.1 0.8 %copy.15 = f32[1,1,16,64,64]{4,3,2,1,0:T(8,128)} copy(f32[1,1,16,64,64]{4,3,2,1,0:T(8,128)S(1)} %bitcast.3) | data formatting | bytes 524288

commit v6 on v5

--- a/solution.py
+++ b/solution.py
@@ -10,7 +10,7 @@
 MESH = pl.DeviceIdType.MESH
 F32, BF16 = jnp.float32, jnp.bfloat16
 LANES = 128
-PIVOTS = 4
+PIVOTS = 8
 ROUNDS = 9
 PITCH = 72
 COARSE_ROUNDS = (7,)

time: 71 us -> 70.2 us (0.989)
    pallas_call x1, Pallas kernels: 68.2 us -> 67.5 us  [body(): pl.pallas_call(functools.partial(kernel, n_row, n_col), out_shape=(jax.Sh...]
where the time goes in v6:
time: 70.2 us; the launch traced here: 70.1 us
  Pallas kernels  67.5 us (96%)
  local copies, waits for them, and re-layouts  2.02 us (3%)
    pallas_call x1, Pallas kernels, body(): pl.pallas_call(functools.partial(kernel, n_row, n_col), out_shape=(jax.Sh...  67.5 us
    unnamed x3, local copies, waits for them, and re-layouts  2.02 us

profile of v6, /device:TPU:1, one launch (start us, length us, event | category | flops | bytes accessed | tf_op | source)
XLA Modules:
  0.0 70.1 jit_solution(10438205984966327808)
XLA Ops:
  0.6 67.5 %deflated_cg.1 = (f32[4,16,128]{2,1,0:T(8,128)S(1)}, f32[4,16,128]{2,1,0:T(8,128)S(1)}, f32[16,64,64]{2,1,0:T(8,128)S(1)}) custom-call(f32[8]{0:T(128)} %cap_ref.1, f32[8]{0:T(128)} %con_ref.1, s32[2]{0:T(128)} %bitcast.5, f32[4,16,128]{2,1,0:T(8,128)} %rhs_hbm.1, s32[4,16,128]{2,1,0:T(8,128)} %mat_hbm.1, f32[16,128]{1,0:T(8,128)} %vent_hbm.1, ...), custom_call_target="tpu_custom_call" | custom-call | tf_op jit(solution)/shard_map/deflated_cg/pallas_call | solution.py:679
  68.1 0.6 copy.13
  68.7 0.6 copy.14
  69.4 0.8 %copy.15 = f32[1,1,16,64,64]{4,3,2,1,0:T(8,128)} copy(f32[1,1,16,64,64]{4,3,2,1,0:T(8,128)S(1)} %bitcast.3) | data formatting | bytes 524288
